TPU v7x, 512 devices: a whole 4x8x8 slice. The times are simulated.
512 devices in a mesh: lat: 32 (over x_hi, y, core), lon: 16 (over z, x_lo).
Axes of the slice: x: 4 (x_hi: 2, x_lo: 2; x = x_hi * 2 + x_lo), y: 8, z: 8, core: 2. Of those that a mesh axis runs over, the one named last changes fastest.
Arguments:
- features: bfloat16 [512, 1024, 128], P('lat', 'lon'), may hold values from -6 to 6
- w_first: bfloat16 [2, 1, 128, 128], replicated, may hold values from -0.375 to 0.375
- bias_first: float32 [2, 1, 128], replicated, may hold values from -3 to 3
- w_second: bfloat16 [2, 1, 128, 128], replicated, may hold values from -0.375 to 0.375
- bias_second: float32 [2, 1, 128], replicated, may hold values from -0.3 to 0.3
Outputs:
- mixed_field: bfloat16 [512, 1024, 128], P('lat', 'lon')
All inputs are finite; a program needn't handle non-finite values.
Results may differ from a plain program's by a relative error of at most 0.025.
Values may be sent and summed in bfloat16 or wider, within the bound.
A program may use at most 64 MiB of HBM per device.

v0:
```python
import math

import jax
import jax.numpy as jnp
from jax import lax
from jax.sharding import PartitionSpec as P

shrink_level = 0.01


def phase_pair(product, length, sign):
    angle_value = (product % length).astype(jnp.float32) * (sign * 2.0 * math.pi / length)
    return (jnp.cos(angle_value), jnp.sin(angle_value))


def index_outer(left_index, right_index):
    return left_index[:, None] * right_index[None, :]


def twin_dot(pattern, operand, phase_table):
    upper_part = phase_table.astype(jnp.bfloat16)
    lower_part = (phase_table - upper_part.astype(jnp.float32)).astype(jnp.bfloat16)
    return jnp.einsum(
        pattern, operand, upper_part, preferred_element_type=jnp.float32
    ) + jnp.einsum(pattern, operand, lower_part, preferred_element_type=jnp.float32)


def complex_table(pattern, real_part, imag_part, cos_table, sin_table):
    real_out = twin_dot(pattern, real_part, cos_table) - twin_dot(pattern, imag_part, sin_table)
    imag_out = twin_dot(pattern, real_part, sin_table) + twin_dot(pattern, imag_part, cos_table)
    return (real_out, imag_out)


def bit_reverse(number, levels):
    result = jnp.zeros_like(number)
    for bit_level in range(levels):
        result = result + number // 2**bit_level % 2 * 2 ** (levels - 1 - bit_level)
    return result


def local_sections(received, levels):
    full_shape = received.shape
    real_part = received.astype(jnp.float32)
    imag_part = jnp.zeros_like(real_part)
    real_half = received
    imag_half = imag_part.astype(jnp.bfloat16)
    for section_level in range(levels - 1, -1, -1):
        half_span = 2**section_level
        split_shape = (full_shape[0], full_shape[1] // (2 * half_span), 2, half_span) + full_shape[
            2:
        ]
        real_split = real_part.reshape(split_shape)
        imag_split = imag_part.reshape(split_shape)
        tw_cos, tw_sin = phase_pair(jnp.arange(half_span, dtype=jnp.int32), 2 * half_span, -1.0)
        tw_cos = tw_cos[None, None, :, None, None]
        tw_sin = tw_sin[None, None, :, None, None]
        sum_re = real_split[:, :, 0] + real_split[:, :, 1]
        sum_im = imag_split[:, :, 0] + imag_split[:, :, 1]
        diff_re = real_split[:, :, 0] - real_split[:, :, 1]
        diff_im = imag_split[:, :, 0] - imag_split[:, :, 1]
        upper_re = diff_re * tw_cos - diff_im * tw_sin
        upper_im = diff_re * tw_sin + diff_im * tw_cos
        real_half = jnp.stack([sum_re, upper_re], axis=2).reshape(full_shape).astype(jnp.bfloat16)
        imag_half = jnp.stack([sum_im, upper_im], axis=2).reshape(full_shape).astype(jnp.bfloat16)
        real_part = real_half.astype(jnp.float32)
        imag_part = imag_half.astype(jnp.float32)
    return (real_half, imag_half)


def block_product(real_part, imag_part, weights):
    real_out = jnp.einsum(
        "tnj,njk->tnk", real_part, weights[0], preferred_element_type=jnp.float32
    ) - jnp.einsum("tnj,njk->tnk", imag_part, weights[1], preferred_element_type=jnp.float32)
    imag_out = jnp.einsum(
        "tnj,njk->tnk", imag_part, weights[0], preferred_element_type=jnp.float32
    ) + jnp.einsum("tnj,njk->tnk", real_part, weights[1], preferred_element_type=jnp.float32)
    return (real_out, imag_out)


def soft_shrink(values):
    return jnp.sign(values) * jnp.maximum(jnp.abs(values) - shrink_level, 0.0)


def spectral_mix(real_part, imag_part, w_first, bias_first, w_second, bias_second):
    hid_re, hid_im = block_product(real_part, imag_part, w_first)
    act_re = jax.nn.relu(hid_re + bias_first[0]).astype(jnp.bfloat16)
    act_im = jax.nn.relu(hid_im + bias_first[1]).astype(jnp.bfloat16)
    out_re, out_im = block_product(act_re, act_im, w_second)
    return (
        soft_shrink(out_re + bias_second[0]).astype(jnp.bfloat16),
        soft_shrink(out_im + bias_second[1]).astype(jnp.bfloat16),
    )


def send_real(blocks):
    return lax.all_to_all(blocks, "lon", split_axis=1, concat_axis=1, tiled=True)


def to_columns(real_part, imag_part):
    return (
        lax.all_to_all(real_part, "lat", split_axis=1, concat_axis=0, tiled=True),
        lax.all_to_all(imag_part, "lat", split_axis=1, concat_axis=0, tiled=True),
    )


def to_rows(real_part, imag_part):
    return (
        lax.all_to_all(real_part, "lat", split_axis=0, concat_axis=1, tiled=True),
        lax.all_to_all(imag_part, "lat", split_axis=0, concat_axis=1, tiled=True),
    )


def body(features, w_first, bias_first, w_second, bias_second):
    lat_rows, lon_cells, channels = features.shape
    lon_count = lax.axis_size("lon")
    lat_count = lax.axis_size("lat")
    total_lat = lat_rows * lat_count
    total_lon = lon_cells * lon_count
    stride = lon_cells // lon_count
    keep_cells = lon_cells // 2
    norm_factor = 1.0 / math.sqrt(total_lat * total_lon)
    levels = lon_count.bit_length() - 1
    lon_place = lax.axis_index("lon")
    shard_index = jnp.arange(lon_count, dtype=jnp.int32)
    cell_index = jnp.arange(lon_cells, dtype=jnp.int32)
    keep_index = jnp.arange(keep_cells, dtype=jnp.int32)
    own_freq = bit_reverse(lon_place, levels)
    source_freq = bit_reverse(shard_index, levels)
    received = send_real(features.reshape(lat_rows, lon_count, stride, channels))
    sectioned_re, sectioned_im = local_sections(received, levels)
    cell_local = lon_place * stride + jnp.arange(stride, dtype=jnp.int32)
    rot_cos, rot_sin = phase_pair(index_outer(source_freq, cell_local), total_lon, -1.0)
    rot_cos = rot_cos[None, :, :, None]
    rot_sin = rot_sin[None, :, :, None]
    section_re = sectioned_re.astype(jnp.float32)
    section_im = sectioned_im.astype(jnp.float32)
    first_re = (section_re * rot_cos - section_im * rot_sin).astype(jnp.bfloat16)
    first_im = (section_re * rot_sin + section_im * rot_cos).astype(jnp.bfloat16)
    first_re, first_im = (
        lax.all_to_all(first_re, "lon", split_axis=1, concat_axis=1, tiled=True),
        lax.all_to_all(first_im, "lon", split_axis=1, concat_axis=1, tiled=True),
    )
    first_re = first_re.reshape(lat_rows, lon_cells, channels)
    first_im = first_im.reshape(lat_rows, lon_cells, channels)
    wave_cos, wave_sin = phase_pair(index_outer(cell_index, keep_index), lon_cells, -1.0)
    lon_re, lon_im = complex_table("rmc,mq->rqc", first_re, first_im, wave_cos, wave_sin)
    col_re, col_im = to_columns(lon_re.astype(jnp.bfloat16), lon_im.astype(jnp.bfloat16))
    row_index = jnp.arange(total_lat, dtype=jnp.int32)
    lat_cos, lat_sin = phase_pair(index_outer(row_index, row_index), total_lat, -1.0)
    spec_re, spec_im = complex_table("rqc,rl->lqc", col_re, col_im, lat_cos, lat_sin)
    spec_re = (spec_re * norm_factor).astype(jnp.bfloat16)
    spec_im = (spec_im * norm_factor).astype(jnp.bfloat16)
    mix_re, mix_im = spectral_mix(spec_re, spec_im, w_first, bias_first, w_second, bias_second)
    back_re, back_im = complex_table("lqc,lr->rqc", mix_re, mix_im, lat_cos, -lat_sin)
    back_re, back_im = to_rows(back_re.astype(jnp.bfloat16), back_im.astype(jnp.bfloat16))
    mode_weight = jnp.where((own_freq == 0) & (keep_index == 0), 1.0, 2.0).astype(jnp.float32)
    inv_cos, inv_sin = phase_pair(index_outer(keep_index, cell_index), lon_cells, 1.0)
    inv_cos = inv_cos * mode_weight[:, None]
    inv_sin = inv_sin * mode_weight[:, None]
    inv_re, inv_im = complex_table("rqc,qm->rmc", back_re, back_im, inv_cos, inv_sin)
    turn_cos, turn_sin = phase_pair(cell_index * own_freq, total_lon, 1.0)
    turn_cos = turn_cos[None, :, None]
    turn_sin = turn_sin[None, :, None]
    lon_back_re = (inv_re * turn_cos - inv_im * turn_sin).astype(jnp.bfloat16)
    lon_back_im = (inv_re * turn_sin + inv_im * turn_cos).astype(jnp.bfloat16)
    lon_back_re = lon_back_re.reshape(lat_rows, lon_count, stride, channels)
    lon_back_im = lon_back_im.reshape(lat_rows, lon_count, stride, channels)
    got_re, got_im = (
        lax.all_to_all(lon_back_re, "lon", split_axis=1, concat_axis=1, tiled=True),
        lax.all_to_all(lon_back_im, "lon", split_axis=1, concat_axis=1, tiled=True),
    )
    back_cos, back_sin = phase_pair(index_outer(source_freq, shard_index), lon_count, 1.0)
    spatial = twin_dot("rxsc,xb->rbsc", got_re, back_cos) - twin_dot(
        "rxsc,xb->rbsc", got_im, back_sin
    )
    filtered = (spatial * norm_factor).astype(jnp.bfloat16)
    filtered = send_real(filtered).reshape(lat_rows, lon_cells, channels)
    return (features.astype(jnp.float32) + filtered.astype(jnp.float32)).astype(jnp.bfloat16)


def solution(mesh):
    in_specs = (P("lat", "lon", None), P(), P(), P(), P())
    out_specs = P("lat", "lon", None)
    return jax.shard_map(body, mesh=mesh, in_specs=in_specs, out_specs=out_specs, check_vma=False)
```

profile of v0, /device:TPU:1, one launch (start us, length us, event | category | flops | bytes accessed | tf_op | source)
XLA Modules:
  0.0 243.0 jit_solution(9135461350170942632)
XLA Ops:
  0.0 1.8 copy.37
  1.8 11.9 %all-to-all-start = ((bf16[16,16,4,128]{3,2,0,1:T(4,128)(2,1)}), bf16[16,16,4,128]{3,2,0,1:T(4,128)(2,1)S(1)}, u32[]{:S(2)}, u32[]{:S(2)}) async-start(bf16[16,16,4,128]{3,2,0,1:T(4,128)(2,1)} %copy.37), calls=%async_computation | async-start | bytes 524288 | tf_op jit(solution)/shard_map/all_to_all | solution.py:96
  14.2 10.0 %all-to-all-done = bf16[16,16,4,128]{3,2,0,1:T(4,128)(2,1)S(1)} async-done(((bf16[16,16,4,128]{3,2,0,1:T(4,128)(2,1)}), bf16[16,16,4,128]{3,2,0,1:T(4,128)(2,1)S(1)}, u32[]{:S(2)}, u32[]{:S(2)}) %all-to-all-start) | async-done | bytes 262176 | tf_op jit(solution)/shard_map/all_to_all | solution.py:96
  27.2 1.2 fusion.47
  28.4 3.5 %all-to-all-start.1 = ((bf16[16,16,4,128]{3,2,0,1:T(4,128)(2,1)}), bf16[16,16,4,128]{3,2,0,1:T(4,128)(2,1)S(1)}, u32[]{:S(2)}, u32[]{:S(2)}) async-start(bf16[16,16,4,128]{3,2,0,1:T(4,128)(2,1)} %get-tuple-element.14), calls=%async_computation.1 | async-start | bytes 524288 | tf_op jit(solution)/shard_map/all_to_all | solution.py:140
  32.0 0.7 copy-done.3
  32.6 0.7 copy-done.4
  33.3 8.2 %all-to-all-done.1 = bf16[16,16,4,128]{3,2,0,1:T(4,128)(2,1)S(1)} async-done(((bf16[16,16,4,128]{3,2,0,1:T(4,128)(2,1)}), bf16[16,16,4,128]{3,2,0,1:T(4,128)(2,1)S(1)}, u32[]{:S(2)}, u32[]{:S(2)}) %all-to-all-start.1) | async-done | bytes 262176 | tf_op jit(solution)/shard_map/all_to_all | solution.py:140
  41.5 3.5 %all-to-all-start.2 = ((bf16[16,16,4,128]{3,2,0,1:T(4,128)(2,1)}), bf16[16,16,4,128]{3,2,0,1:T(4,128)(2,1)S(1)}, u32[]{:S(2)}, u32[]{:S(2)}) async-start(bf16[16,16,4,128]{3,2,0,1:T(4,128)(2,1)} %get-tuple-element.13), calls=%async_computation.2 | async-start | bytes 524288 | tf_op jit(solution)/shard_map/all_to_all | solution.py:141
  45.9 8.8 %all-to-all-done.2 = bf16[16,16,4,128]{3,2,0,1:T(4,128)(2,1)S(1)} async-done(((bf16[16,16,4,128]{3,2,0,1:T(4,128)(2,1)}), bf16[16,16,4,128]{3,2,0,1:T(4,128)(2,1)S(1)}, u32[]{:S(2)}, u32[]{:S(2)}) %all-to-all-start.2) | async-done | bytes 262176 | tf_op jit(solution)/shard_map/all_to_all | solution.py:141
  55.3 0.7 copy.41
  56.1 14.3 %all-to-all-start.4 = ((bf16[16,32,128]{2,0,1:T(8,128)(2,1)}), bf16[16,32,128]{2,0,1:T(8,128)(2,1)S(1)}, u32[]{:S(2)}, u32[]{:S(2)}) async-start(bf16[16,32,128]{2,0,1:T(8,128)(2,1)} %copy.41), calls=%async_computation.4 | async-start | bytes 262144 | tf_op jit(solution)/shard_map/all_to_all | solution.py:102
  71.1 0.7 copy.40
  71.8 9.1 %all-to-all-done.4 = bf16[16,32,128]{2,0,1:T(8,128)(2,1)S(1)} async-done(((bf16[16,32,128]{2,0,1:T(8,128)(2,1)}), bf16[16,32,128]{2,0,1:T(8,128)(2,1)S(1)}, u32[]{:S(2)}, u32[]{:S(2)}) %all-to-all-start.4) | async-done | bytes 131104 | tf_op jit(solution)/shard_map/all_to_all | solution.py:102
  80.9 5.1 %all-to-all-start.3 = ((bf16[16,32,128]{2,0,1:T(8,128)(2,1)}), bf16[16,32,128]{2,0,1:T(8,128)(2,1)S(1)}, u32[]{:S(2)}, u32[]{:S(2)}) async-start(bf16[16,32,128]{2,0,1:T(8,128)(2,1)} %copy.40), calls=%async_computation.3 | async-start | bytes 262144 | tf_op jit(solution)/shard_map/all_to_all | solution.py:101
  86.0 4.7 %fusion.57 = f32[512,128]{1,0:T(8,128)S(1)} fusion(bf16[512,128]{1,0:T(8,128)(2,1)S(1)} %bitcast.282), kind=kOutput, calls=%fused_computation.91 | convolution fusion | flops 71041024 | bytes 393216 | tf_op jit(solution)/shard_map/rqc,rl->lqc/dot_general | solution.py:23
  90.7 4.7 %fusion.63 = f32[512,128]{1,0:T(8,128)S(1)} fusion(bf16[512,128]{1,0:T(8,128)(2,1)S(1)} %bitcast.283), kind=kOutput, calls=%fused_computation.94 | convolution fusion | flops 71041024 | bytes 393216 | tf_op jit(solution)/shard_map/rqc,rl->lqc/dot_general | solution.py:23
  95.5 1.2 all-to-all-done.3
  96.7 4.7 %fusion.61 = f32[512,128]{1,0:T(8,128)S(1)} fusion(bf16[512,128]{1,0:T(8,128)(2,1)S(1)} %bitcast.286), kind=kOutput, calls=%fused_computation.93 | convolution fusion | flops 71041024 | bytes 393216 | tf_op jit(solution)/shard_map/rqc,rl->lqc/dot_general | solution.py:23
  101.4 4.7 %fusion.59 = f32[512,128]{1,0:T(8,128)S(1)} fusion(bf16[512,128]{1,0:T(8,128)(2,1)S(1)} %bitcast.287), kind=kOutput, calls=%fused_computation.92 | convolution fusion | flops 71041024 | bytes 393216 | tf_op jit(solution)/shard_map/rqc,rl->lqc/dot_general | solution.py:23
  106.1 4.7 %convolution_add_fusion.12 = f32[512,128]{1,0:T(8,128)S(1)} fusion(f32[512,128]{1,0:T(8,128)S(1)} %fusion.57, bf16[512,128]{1,0:T(8,128)(2,1)S(1)} %bitcast.284), kind=kOutput, calls=%fused_computation.26 | convolution fusion | flops 71892992 | bytes 655360 | tf_op jit(solution)/shard_map/rqc,rl->lqc/dot_general | solution.py:25
  110.8 4.8 %convolution_add_fusion.14 = f32[512,128]{1,0:T(8,128)S(1)} fusion(f32[512,128]{1,0:T(8,128)S(1)} %fusion.63, bf16[512,128]{1,0:T(8,128)(2,1)S(1)} %bitcast.285), kind=kOutput, calls=%fused_computation.28 | convolution fusion | flops 71892992 | bytes 655360 | tf_op jit(solution)/shard_map/rqc,rl->lqc/dot_general | solution.py:25
  115.6 4.8 %fusion.31 = bf16[512,128]{1,0:T(8,128)(2,1)S(1)} fusion(f32[512,128]{1,0:T(8,128)S(1)} %convolution_add_fusion.12, f32[512,128]{1,0:T(8,128)S(1)} %fusion.61, bf16[512,128]{1,0:T(8,128)(2,1)S(1)} %bitcast.288), kind=kOutput, calls=%fused_computation.56 | convolution fusion | flops 72089600 | bytes 786432 | tf_op jit(solution)/shard_map/rqc,rl->lqc/dot_general | solution.py:25
  120.6 4.7 %fusion.30 = bf16[512,128]{1,0:T(8,128)(2,1)S(1)} fusion(f32[512,128]{1,0:T(8,128)S(1)} %convolution_add_fusion.14, f32[512,128]{1,0:T(8,128)S(1)} %fusion.59, bf16[512,128]{1,0:T(8,128)(2,1)S(1)} %bitcast.289), kind=kOutput, calls=%fused_computation.55 | convolution fusion | flops 72089600 | bytes 786432 | tf_op jit(solution)/shard_map/rqc,rl->lqc/dot_general | solution.py:25
  127.1 4.7 %fusion.53 = f32[512,128]{1,0:T(8,128)S(1)} fusion(bf16[512,128]{1,0:T(8,128)(2,1)S(1)} %fusion.67), kind=kOutput, calls=%fused_computation.89 | convolution fusion | flops 71041024 | bytes 393216 | tf_op jit(solution)/shard_map/lqc,lr->rqc/dot_general | solution.py:23
  131.8 4.8 %fusion.66 = f32[512,128]{1,0:T(8,128)S(1)} fusion(bf16[512,128]{1,0:T(8,128)(2,1)S(1)} %fusion.67), kind=kOutput, calls=%fused_computation.96 | convolution fusion | flops 71303168 | bytes 393216 | tf_op jit(solution)/shard_map/lqc,lr->rqc/dot_general | solution.py:23
  136.8 5.0 %fusion.65 = f32[512,128]{1,0:T(8,128)S(1)} fusion(bf16[512,128]{1,0:T(8,128)(2,1)S(1)} %fusion.68), kind=kOutput, calls=%fused_computation.95 | convolution fusion | flops 71303168 | bytes 393216 | tf_op jit(solution)/shard_map/lqc,lr->rqc/dot_general | solution.py:23
  141.8 4.7 %fusion.55 = f32[512,128]{1,0:T(8,128)S(1)} fusion(bf16[512,128]{1,0:T(8,128)(2,1)S(1)} %fusion.68), kind=kOutput, calls=%fused_computation.90 | convolution fusion | flops 71041024 | bytes 393216 | tf_op jit(solution)/shard_map/lqc,lr->rqc/dot_general | solution.py:23
  146.5 4.7 %convolution_add_fusion.6 = f32[512,128]{1,0:T(8,128)S(1)} fusion(f32[512,128]{1,0:T(8,128)S(1)} %fusion.53, bf16[512,128]{1,0:T(8,128)(2,1)S(1)} %fusion.67), kind=kOutput, calls=%fused_computation.14 | convolution fusion | flops 71892992 | bytes 655360 | tf_op jit(solution)/shard_map/lqc,lr->rqc/dot_general | solution.py:25
  151.3 4.8 %fusion.37 = bf16[512,1,128]{2,0,1:T(8,128)(2,1)S(1)} fusion(f32[512,128]{1,0:T(8,128)S(1)} %convolution_add_fusion.6, f32[512,128]{1,0:T(8,128)S(1)} %fusion.65, bf16[512,128]{1,0:T(8,128)(2,1)S(1)} %fusion.68), kind=kOutput, calls=%fused_computation.62 | convolution fusion | flops 72286208 | bytes 786432 | tf_op jit(solution)/shard_map/lqc,lr->rqc/dot_general | solution.py:25
  156.7 0.7 reduce
  157.4 0.7 reshape.551
  158.1 8.7 %all-to-all-start.6 = ((bf16[32,2,1024]{2,1,0:T(2,128)(2,1)}), bf16[32,2,1024]{2,1,0:T(2,128)(2,1)S(1)}, u32[]{:S(2)}, u32[]{:S(2)}) async-start(bf16[32,2,1024]{2,1,0:T(2,128)(2,1)} %reshape.551), calls=%async_computation.6 | async-start | bytes 262144 | tf_op jit(solution)/shard_map/all_to_all | solution.py:109
  166.8 4.8 %convolution_add_fusion.8 = f32[512,128]{1,0:T(8,128)S(1)} fusion(f32[512,128]{1,0:T(8,128)S(1)} %fusion.66, bf16[512,128]{1,0:T(8,128)(2,1)S(1)} %fusion.67), kind=kOutput, calls=%fused_computation.16 | convolution fusion | flops 72155136 | bytes 655360 | tf_op jit(solution)/shard_map/lqc,lr->rqc/dot_general | solution.py:25
  171.6 4.7 %fusion.36 = bf16[512,1,128]{2,0,1:T(8,128)(2,1)S(1)} fusion(f32[512,128]{1,0:T(8,128)S(1)} %convolution_add_fusion.8, f32[512,128]{1,0:T(8,128)S(1)} %fusion.55, bf16[512,128]{1,0:T(8,128)(2,1)S(1)} %fusion.68), kind=kOutput, calls=%fused_computation.61 | convolution fusion | flops 72024064 | bytes 786432 | tf_op jit(solution)/shard_map/lqc,lr->rqc/dot_general | solution.py:25
  176.3 0.7 reduce.1
  177.1 0.7 reshape.553
  177.7 9.8 %all-to-all-start.5 = ((bf16[32,2,1024]{2,1,0:T(2,128)(2,1)}), bf16[32,2,1024]{2,1,0:T(2,128)(2,1)S(1)}, u32[]{:S(2)}, u32[]{:S(2)}) async-start(bf16[32,2,1024]{2,1,0:T(2,128)(2,1)} %reshape.553), calls=%async_computation.5 | async-start | bytes 262144 | tf_op jit(solution)/shard_map/all_to_all | solution.py:108
  188.4 9.8 %all-to-all-done.5 = bf16[32,2,1024]{2,1,0:T(2,128)(2,1)S(1)} async-done(((bf16[32,2,1024]{2,1,0:T(2,128)(2,1)}), bf16[32,2,1024]{2,1,0:T(2,128)(2,1)S(1)}, u32[]{:S(2)}, u32[]{:S(2)}) %all-to-all-start.5) | async-done | bytes 131104 | tf_op jit(solution)/shard_map/all_to_all | solution.py:108
  200.4 0.8 copy.49
  201.2 3.5 %all-to-all-start.8 = ((bf16[16,16,4,128]{3,2,0,1:T(4,128)(2,1)}), bf16[16,16,4,128]{3,2,0,1:T(4,128)(2,1)S(1)}, u32[]{:S(2)}, u32[]{:S(2)}) async-start(bf16[16,16,4,128]{3,2,0,1:T(4,128)(2,1)} %copy.49), calls=%async_computation.8 | async-start | bytes 524288 | tf_op jit(solution)/shard_map/all_to_all | solution.py:170
  204.8 0.8 copy.46
  205.6 8.9 %all-to-all-done.8 = bf16[16,16,4,128]{3,2,0,1:T(4,128)(2,1)S(1)} async-done(((bf16[16,16,4,128]{3,2,0,1:T(4,128)(2,1)}), bf16[16,16,4,128]{3,2,0,1:T(4,128)(2,1)S(1)}, u32[]{:S(2)}, u32[]{:S(2)}) %all-to-all-start.8) | async-done | bytes 262176 | tf_op jit(solution)/shard_map/all_to_all | solution.py:170
  214.5 3.8 %all-to-all-start.7 = ((bf16[16,16,4,128]{3,2,0,1:T(4,128)(2,1)}), bf16[16,16,4,128]{3,2,0,1:T(4,128)(2,1)S(1)}, u32[]{:S(2)}, u32[]{:S(2)}) async-start(bf16[16,16,4,128]{3,2,0,1:T(4,128)(2,1)} %copy.46), calls=%async_computation.7 | async-start | bytes 524288 | tf_op jit(solution)/shard_map/all_to_all | solution.py:169
  219.0 9.0 %all-to-all-done.7 = bf16[16,16,4,128]{3,2,0,1:T(4,128)(2,1)S(1)} async-done(((bf16[16,16,4,128]{3,2,0,1:T(4,128)(2,1)}), bf16[16,16,4,128]{3,2,0,1:T(4,128)(2,1)S(1)}, u32[]{:S(2)}, u32[]{:S(2)}) %all-to-all-start.7) | async-done | bytes 262176 | tf_op jit(solution)/shard_map/all_to_all | solution.py:169
  228.7 12.3 %all_to_all.96 = bf16[16,16,4,128]{3,2,0,1:T(4,128)(2,1)S(1)} all-to-all(bf16[16,16,4,128]{3,2,0,1:T(4,128)(2,1)S(1)} %copy.52), channel_id=1, replica_groups=mesh['lat'=32,'lon'=16] {'lon'}, dimensions={1} | all-to-all | bytes 524288 | tf_op jit(solution)/shard_map/all_to_all | solution.py:96
  241.1 0.9 copy-done
  242.2 0.8 copy.54
  (76 shorter events, 12.8 us)
Async XLA Ops:
  1.8 22.4 %all-to-all-start = ((bf16[16,16,4,128]{3,2,0,1:T(4,128)(2,1)}), bf16[16,16,4,128]{3,2,0,1:T(4,128)(2,1)S(1)}, u32[]{:S(2)}, u32[]{:S(2)}) async-start(bf16[16,16,4,128]{3,2,0,1:T(4,128)(2,1)} %copy.37), calls=%async_computation | async-start | bytes 524288 | tf_op jit(solution)/shard_map/all_to_all | solution.py:96
  28.4 13.1 %all-to-all-start.1 = ((bf16[16,16,4,128]{3,2,0,1:T(4,128)(2,1)}), bf16[16,16,4,128]{3,2,0,1:T(4,128)(2,1)S(1)}, u32[]{:S(2)}, u32[]{:S(2)}) async-start(bf16[16,16,4,128]{3,2,0,1:T(4,128)(2,1)} %get-tuple-element.14), calls=%async_computation.1 | async-start | bytes 524288 | tf_op jit(solution)/shard_map/all_to_all | solution.py:140
  31.9 0.7 copy-start.3
  32.6 0.7 copy-start.4
  41.5 13.2 %all-to-all-start.2 = ((bf16[16,16,4,128]{3,2,0,1:T(4,128)(2,1)}), bf16[16,16,4,128]{3,2,0,1:T(4,128)(2,1)S(1)}, u32[]{:S(2)}, u32[]{:S(2)}) async-start(bf16[16,16,4,128]{3,2,0,1:T(4,128)(2,1)} %get-tuple-element.13), calls=%async_computation.2 | async-start | bytes 524288 | tf_op jit(solution)/shard_map/all_to_all | solution.py:141
  56.1 24.8 %all-to-all-start.4 = ((bf16[16,32,128]{2,0,1:T(8,128)(2,1)}), bf16[16,32,128]{2,0,1:T(8,128)(2,1)S(1)}, u32[]{:S(2)}, u32[]{:S(2)}) async-start(bf16[16,32,128]{2,0,1:T(8,128)(2,1)} %copy.41), calls=%async_computation.4 | async-start | bytes 262144 | tf_op jit(solution)/shard_map/all_to_all | solution.py:102
  80.9 15.8 %all-to-all-start.3 = ((bf16[16,32,128]{2,0,1:T(8,128)(2,1)}), bf16[16,32,128]{2,0,1:T(8,128)(2,1)S(1)}, u32[]{:S(2)}, u32[]{:S(2)}) async-start(bf16[16,32,128]{2,0,1:T(8,128)(2,1)} %copy.40), calls=%async_computation.3 | async-start | bytes 262144 | tf_op jit(solution)/shard_map/all_to_all | solution.py:101
  115.6 4.8 %copy-start.1 = (bf16[2,1,128,128]{3,2,1,0:T(8,128)(2,1)S(1)}, bf16[2,1,128,128]{3,2,1,0:T(8,128)(2,1)}, u32[]{:S(2)}) copy-start(bf16[2,1,128,128]{3,2,1,0:T(8,128)(2,1)} %param.6) | copy-start | bytes 196612
  125.5 0.8 copy-start.2
  158.1 19.7 %all-to-all-start.6 = ((bf16[32,2,1024]{2,1,0:T(2,128)(2,1)}), bf16[32,2,1024]{2,1,0:T(2,128)(2,1)S(1)}, u32[]{:S(2)}, u32[]{:S(2)}) async-start(bf16[32,2,1024]{2,1,0:T(2,128)(2,1)} %reshape.551), calls=%async_computation.6 | async-start | bytes 262144 | tf_op jit(solution)/shard_map/all_to_all | solution.py:109
  177.7 20.4 %all-to-all-start.5 = ((bf16[32,2,1024]{2,1,0:T(2,128)(2,1)}), bf16[32,2,1024]{2,1,0:T(2,128)(2,1)S(1)}, u32[]{:S(2)}, u32[]{:S(2)}) async-start(bf16[32,2,1024]{2,1,0:T(2,128)(2,1)} %reshape.553), calls=%async_computation.5 | async-start | bytes 262144 | tf_op jit(solution)/shard_map/all_to_all | solution.py:108
  201.2 13.3 %all-to-all-start.8 = ((bf16[16,16,4,128]{3,2,0,1:T(4,128)(2,1)}), bf16[16,16,4,128]{3,2,0,1:T(4,128)(2,1)S(1)}, u32[]{:S(2)}, u32[]{:S(2)}) async-start(bf16[16,16,4,128]{3,2,0,1:T(4,128)(2,1)} %copy.49), calls=%async_computation.8 | async-start | bytes 524288 | tf_op jit(solution)/shard_map/all_to_all | solution.py:170
  214.5 13.4 %all-to-all-start.7 = ((bf16[16,16,4,128]{3,2,0,1:T(4,128)(2,1)}), bf16[16,16,4,128]{3,2,0,1:T(4,128)(2,1)S(1)}, u32[]{:S(2)}, u32[]{:S(2)}) async-start(bf16[16,16,4,128]{3,2,0,1:T(4,128)(2,1)} %copy.46), calls=%async_computation.7 | async-start | bytes 524288 | tf_op jit(solution)/shard_map/all_to_all | solution.py:169
  241.1 1.0 copy-start
where the time goes:
time: 247 us; the launch traced here: 243 us
  matrix products  83.4 us (34%)
  waiting for transfers between devices  65.1 us (26%)
  starting transfers between devices  64.2 us (26%)
  blocking collectives  12.3 us (5%)
  local copies, waits for them, and re-layouts  11.2 us (5%)
  other arithmetic  6.01 us (2%)
    dot_general x18, matrix products, twin_dot(): jnp.einsum(pattern, operand, lower_part, preferred_element_type=jnp.float32)  41.1 us
    dot_general x18, matrix products, twin_dot(): jnp.einsum(pattern, operand, upper_part, preferred_element_type=jnp.float32)  40.8 us
    all_to_all x1, starting transfers between devices, to_columns(): lax.all_to_all(imag_part, 'lat', split_axis=1, concat_axis=0, tiled=True)  14.3 us
    all_to_all x1, blocking collectives, send_real(): lax.all_to_all(blocks, 'lon', split_axis=1, concat_axis=1, tiled=True)  12.3 us
    all_to_all x1, starting transfers between devices, send_real(): lax.all_to_all(blocks, 'lon', split_axis=1, concat_axis=1, tiled=True)  11.9 us
    all_to_all x1, waiting for transfers between devices, send_real(): lax.all_to_all(blocks, 'lon', split_axis=1, concat_axis=1, tiled=True)  10 us
    all_to_all x1, starting transfers between devices, to_rows(): lax.all_to_all(real_part, 'lat', split_axis=0, concat_axis=1, tiled=True)  9.82 us
    all_to_all x1, waiting for transfers between devices, to_rows(): lax.all_to_all(real_part, 'lat', split_axis=0, concat_axis=1, tiled=True)  9.78 us
  transfers between devices with their start and end apart: 9, of which 8 were waited for; matrix products, arithmetic and copies ran while one was open for 10% of the time, Pallas kernels for 0%

commit v1 on v0

v1 whole, which is shorter than its diff:
```python
import functools
import math

import jax
import jax.numpy as jnp
import numpy as np
from jax import lax
from jax.experimental import pallas as pl
from jax.experimental.pallas import tpu as pltpu
from jax.sharding import PartitionSpec as P

shrink_level = 0.01
MESH = pl.DeviceIdType.MESH


def tables(total_lat, total_lon):
    waves = total_lon // 2
    turn = np.outer(np.arange(waves), np.arange(total_lon)) % total_lon
    angle = turn * (2.0 * math.pi / total_lon)
    lon_cos, lon_sin = np.cos(angle), np.sin(angle)
    lon_forward = np.stack([lon_cos, -lon_sin], axis=1).reshape(2 * waves, total_lon)
    weight = np.where(np.arange(waves) == 0, 1.0, 2.0)[:, None]
    lon_inverse = np.stack([weight * lon_cos, -weight * lon_sin], axis=1)
    lon_inverse = lon_inverse.reshape(2 * waves, total_lon).T
    turn = np.outer(np.arange(total_lat), np.arange(total_lat)) % total_lat
    angle = turn * (2.0 * math.pi / total_lat)
    lat_cos, lat_sin = np.cos(angle), np.sin(angle)
    lat_forward = np.zeros((2, total_lat, total_lat, 2))
    lat_forward[0, :, :, 0] = lat_cos
    lat_forward[0, :, :, 1] = lat_sin
    lat_forward[1, :, :, 0] = -lat_sin
    lat_forward[1, :, :, 1] = lat_cos
    lat_forward = lat_forward.reshape(2 * total_lat, 2 * total_lat)
    lat_inverse = lat_forward.T
    return [
        np.ascontiguousarray(t).astype(jnp.bfloat16)
        for t in (lon_forward, lat_forward, lat_inverse, lon_inverse)
    ]


def mixer_kernel(
    lat_count,
    lon_count,
    x_ref,
    t1_hbm,
    t2_hbm,
    t3_hbm,
    t4_hbm,
    w1_ref,
    b1_ref,
    w2_ref,
    b2_ref,
    out_ref,
    t1,
    t2,
    t3,
    t4,
    line,
    spec,
    part,
    column,
    mixed,
    back,
    rows,
    waves,
    field,
    send_sem,
    recv_sem,
    table_sem,
):
    lat = lax.axis_index("lat")
    lon = lax.axis_index("lon")
    cells = x_ref.shape[1]
    norm = 1.0 / math.sqrt(lat_count * x_ref.shape[0] * lon_count * cells)

    table_copies = [
        pltpu.make_async_copy(hbm, vmem, table_sem.at[n])
        for n, (hbm, vmem) in enumerate(((t1_hbm, t1), (t2_hbm, t2), (t3_hbm, t3), (t4_hbm, t4)))
    ]
    for copy in table_copies:
        copy.start()

    barrier = pltpu.get_barrier_semaphore()

    def greet_lon(step, _):
        peer = lax.rem(lon + step, lon_count)
        pl.semaphore_signal(barrier, inc=1, device_id={"lon": peer}, device_id_type=MESH)
        return 0

    def greet_lat(step, _):
        peer = lax.rem(lat + step, lat_count)
        pl.semaphore_signal(barrier, inc=1, device_id={"lat": peer}, device_id_type=MESH)
        return 0

    lax.fori_loop(1, lon_count, greet_lon, 0)
    lax.fori_loop(1, lat_count, greet_lat, 0)
    pl.semaphore_wait(barrier, lon_count + lat_count - 2)

    def exchange(stage, axis, me, count, source, target):
        own = pltpu.make_async_copy(source(me), target, recv_sem.at[stage])
        own.start()

        def send(step, _):
            peer = lax.rem(me + step, count)
            pltpu.make_async_remote_copy(
                src_ref=source(peer),
                dst_ref=target,
                send_sem=send_sem.at[stage],
                recv_sem=recv_sem.at[stage],
                device_id={axis: peer},
                device_id_type=MESH,
            ).start()
            return 0

        lax.fori_loop(1, count, send, 0)

    def arrived(stage, landing):
        pltpu.make_async_copy(landing, landing, recv_sem.at[stage]).wait()

    def aligned(index, size):
        return pl.ds(pl.multiple_of(index * size, size), size)

    exchange(0, "lon", lon, lon_count, lambda p: x_ref.at[p], line.at[aligned(lon, cells)])
    table_copies[0].wait()
    arrived(0, line)
    spec[...] = jnp.dot(t1[...], line[...], preferred_element_type=jnp.float32).astype(spec.dtype)

    exchange(1, "lon", lon, lon_count, lambda p: spec.at[aligned(p, cells)], part.at[lon])
    arrived(1, part)

    exchange(2, "lat", lat, lat_count, lambda p: part.at[:, aligned(p, 2)], column.at[lat])
    table_copies[1].wait()
    arrived(2, column)
    height = t2.shape[0] // 2
    spectrum = jnp.dot(
        t2[...], column.reshape(2 * height, 128)[...], preferred_element_type=jnp.float32
    )
    spectrum = (spectrum * norm).astype(jnp.bfloat16)

    def product(left_re, left_im, w_ref):
        w_re, w_im = w_ref[0, 0], w_ref[1, 0]
        re = jnp.dot(left_re, w_re, preferred_element_type=jnp.float32) - jnp.dot(
            left_im, w_im, preferred_element_type=jnp.float32
        )
        im = jnp.dot(left_im, w_re, preferred_element_type=jnp.float32) + jnp.dot(
            left_re, w_im, preferred_element_type=jnp.float32
        )
        return re, im

    def shrink(v):
        return jnp.maximum(v - shrink_level, 0.0) + jnp.minimum(v + shrink_level, 0.0)

    hid_re, hid_im = product(spectrum[:height], spectrum[height:], w1_ref)
    act_re = jnp.maximum(hid_re + b1_ref[0], 0.0).astype(jnp.bfloat16)
    act_im = jnp.maximum(hid_im + b1_ref[1], 0.0).astype(jnp.bfloat16)
    out_re, out_im = product(act_re, act_im, w2_ref)
    mixed[:height] = shrink(out_re + b2_ref[0]).astype(jnp.bfloat16)
    mixed[height:] = shrink(out_im + b2_ref[1]).astype(jnp.bfloat16)
    table_copies[2].wait()
    back[...] = jnp.dot(t3[...], mixed[...], preferred_element_type=jnp.float32).astype(back.dtype)

    exchange(3, "lat", lat, lat_count, lambda p: back.at[aligned(p, 32)], rows.at[lat])
    arrived(3, rows)

    exchange(4, "lon", lon, lon_count, lambda p: rows.at[:, aligned(p, 2)], waves.at[lon])
    table_copies[3].wait()
    arrived(4, waves)
    filtered = jnp.dot(
        t4[...], waves.reshape(t4.shape[1], 128)[...], preferred_element_type=jnp.float32
    )
    field[...] = (filtered * norm).astype(field.dtype)

    exchange(5, "lon", lon, lon_count, lambda p: field.at[aligned(p, cells)], out_ref.at[lon])
    arrived(5, out_ref)

    for stage, (buffer, count) in enumerate(
        ((line, lon_count), (line, lon_count), (line, lat_count), (line, lat_count), (line, lon_count), (line, lon_count))
    ):
        sent = line.shape[0] // count * (count - 1)
        left = line.at[pl.ds(0, sent)]
        pltpu.make_async_copy(left, left, send_sem.at[stage]).wait()


def body(mesh, features, w_first, bias_first, w_second, bias_second):
    lat_rows, lon_cells, channels = features.shape
    lat_count, lon_count = mesh.shape["lat"], mesh.shape["lon"]
    total_lat, total_lon = lat_rows * lat_count, lon_cells * lon_count
    consts = [jnp.asarray(t) for t in tables(total_lat, total_lon)]
    any_space = pl.BlockSpec(memory_space=pl.ANY)
    vmem = pl.BlockSpec(memory_space=pltpu.VMEM)
    half = jnp.bfloat16
    waves_own = total_lon // 2 // lon_count
    flat = pltpu.VMEM((total_lon, channels), half)
    filtered = pl.pallas_call(
        functools.partial(mixer_kernel, lat_count, lon_count),
        out_shape=jax.ShapeDtypeStruct((lat_rows, lon_cells, channels), half),
        in_specs=[any_space] * 5 + [vmem] * 4,
        out_specs=any_space,
        scratch_shapes=[pltpu.VMEM(t.shape, half) for t in consts]
        + [
            flat,
            flat,
            pltpu.VMEM((lon_count, 2 * waves_own, channels), half),
            pltpu.VMEM((lat_count, lat_rows, 2, channels), half),
            pltpu.VMEM((2 * total_lat, channels), half),
            pltpu.VMEM((2 * total_lat, channels), half),
            pltpu.VMEM((lat_count, 2 * lat_rows, channels), half),
            pltpu.VMEM((lon_count, waves_own, 2, channels), half),
            flat,
            pltpu.SemaphoreType.DMA((6,)),
            pltpu.SemaphoreType.DMA((6,)),
            pltpu.SemaphoreType.DMA((4,)),
        ],
        compiler_params=pltpu.CompilerParams(
            collective_id=0, has_side_effects=True, vmem_limit_bytes=48 * 2**20
        ),
    )(features, *consts, w_first, bias_first, w_second, bias_second)
    return (features.astype(jnp.float32) + filtered.astype(jnp.float32)).astype(features.dtype)


def solution(mesh):
    in_specs = (P("lat", "lon", None), P(), P(), P(), P())
    out_specs = P("lat", "lon", None)
    return jax.shard_map(
        functools.partial(body, mesh),
        mesh=mesh,
        in_specs=in_specs,
        out_specs=out_specs,
        check_vma=False,
    )
```

time: 247 us -> 80.4 us (0.33); the launches traced: 243 us -> 79.9 us
  matrix products: 83.4 us -> 0 us
  Pallas kernels: 0 us -> 71.9 us
  waiting for transfers between devices: 65.1 us -> 0 us
  starting transfers between devices: 64.2 us -> 0 us
  blocking collectives: 12.3 us -> 0 us
  other arithmetic: 6.01 us -> 0.78 us
  local copies, waits for them, and re-layouts: 11.2 us -> 7.17 us
    dot_general x44 -> x0, matrix products: 83.4 us -> none  [the longest x18 41.1 us: twin_dot(): jnp.einsum(pattern, operand, lower_part, preferred_element_type=jnp.float32)]
    pallas_call x0 -> x1, Pallas kernels: none -> 71.9 us  [body(): pl.pallas_call(functools.partial(mixer_kernel, lat_count, lon_count), out...]
    all_to_all x9 -> x0, waiting for transfers between devices: 65.1 us -> none  [the longest x1 10 us: send_real(): lax.all_to_all(blocks, 'lon', split_axis=1, concat_axis=1, tiled=True)]
    all_to_all x9 -> x0, starting transfers between devices: 64.2 us -> none  [the longest x1 14.3 us: to_columns(): lax.all_to_all(imag_part, 'lat', split_axis=1, concat_axis=0, tiled=True)]
    all_to_all x1 -> x0, blocking collectives: 12.3 us -> none  [send_real(): lax.all_to_all(blocks, 'lon', split_axis=1, concat_axis=1, tiled=True)]
    reshape x3 -> x0, local copies, waits for them, and re-layouts: 3.43 us -> none  [the longest x1 1.77 us: body(): features.reshape(lat_rows, lon_count, stride, channels)]
    convert_element_type x5 -> x0, local copies, waits for them, and re-layouts: 2.9 us -> none  [the longest x1 0.77 us: body(): (features.astype(jnp.float32) + filtered.astype(jnp.float32)).astype(jnp....]
    unnamed x16 -> x14, local copies, waits for them, and re-layouts: 4.51 us -> 7.17 us
  transfers between devices with their start and end apart: 9 -> 0, of which waited for: 8 -> 0; matrix products, arithmetic and copies ran while one was open for 10% -> 0% of each run, Pallas kernels for 0% -> 0%
where the time goes in v1:
time: 80.4 us; the launch traced here: 79.9 us
  Pallas kernels  71.9 us (89%)
  local copies, waits for them, and re-layouts  7.17 us (9%)
    pallas_call x1, Pallas kernels, body(): pl.pallas_call(functools.partial(mixer_kernel, lat_count, lon_count), out...  71.9 us
    unnamed x14, local copies, waits for them, and re-layouts  7.17 us

profile of v1, /device:TPU:1, one launch (start us, length us, event | category | flops | bytes accessed | tf_op | source)
XLA Modules:
  0.0 79.9 jit_solution(8932825188364410122)
XLA Ops:
  0.0 0.0 copy-start
  0.0 1.6 %copy-done = bf16[1024,1024]{1,0:T(8,128)(2,1)S(1)} copy-done((bf16[1024,1024]{1,0:T(8,128)(2,1)S(1)}, bf16[1024,1024]{1,0:T(8,128)(2,1)}, u32[]{:S(2)}) %copy-start) | copy-done | bytes 2097176
  1.6 0.0 copy-start.1
  1.6 1.6 %copy-done.1 = bf16[1024,1024]{1,0:T(8,128)(2,1)S(1)} copy-done((bf16[1024,1024]{1,0:T(8,128)(2,1)S(1)}, bf16[1024,1024]{1,0:T(8,128)(2,1)}, u32[]{:S(2)}) %copy-start.1) | copy-done | bytes 2097176
  3.2 0.0 copy-start.2
  3.2 0.9 %copy-done.2 = bf16[16,64,128]{2,1,0:T(8,128)(2,1)S(1)} copy-done((bf16[16,64,128]{2,1,0:T(8,128)(2,1)S(1)}, bf16[16,64,128]{2,1,0:T(8,128)(2,1)}, u32[]{:S(2)}) %copy-start.2) | copy-done | bytes 262168
  4.1 0.0 copy-start.3
  4.1 0.8 %copy-done.3 = bf16[2,1,128,128]{3,2,1,0:T(8,128)(2,1)S(1)} copy-done((bf16[2,1,128,128]{3,2,1,0:T(8,128)(2,1)S(1)}, bf16[2,1,128,128]{3,2,1,0:T(8,128)(2,1)}, u32[]{:S(2)}) %copy-start.3) | copy-done | bytes 65560
  5.0 0.0 copy-start.4
  5.0 0.8 %copy-done.4 = bf16[2,1,128,128]{3,2,1,0:T(8,128)(2,1)S(1)} copy-done((bf16[2,1,128,128]{3,2,1,0:T(8,128)(2,1)S(1)}, bf16[2,1,128,128]{3,2,1,0:T(8,128)(2,1)}, u32[]{:S(2)}) %copy-start.4) | copy-done | bytes 65560
  5.8 0.0 copy-start.5
  5.8 0.7 copy-done.5
  6.5 0.0 copy-start.6
  6.5 0.7 copy-done.6
  7.2 71.9 %shard_map.91 = bf16[16,64,128]{2,1,0:T(8,128)(2,1)S(1)} custom-call(bf16[16,64,128]{2,1,0:T(8,128)(2,1)S(1)} %copy-done.2, bf16[1024,1024]{1,0:T(8,128)(2,1)S(1)} %copy-done.1, bf16[1024,1024]{1,0:T(8,128)(2,1)S(1)} %copy-done, bf16[1024,1024]{1,0:T(8,128)(2,1)} %constant.10.clone.t3_hbm, bf16[1024,1024]{1,0:T(8,128)(2,1)} %constant.11.clone.t4_hbm, ...), custom_call_target="tpu_custom_call" | custom-call | tf_op jit(solution)/shard_map/pallas_call | solution.py:194
  79.1 0.8 add_convert_fusion
Async XLA Ops:
  0.0 1.6 %copy-start = (bf16[1024,1024]{1,0:T(8,128)(2,1)S(1)}, bf16[1024,1024]{1,0:T(8,128)(2,1)}, u32[]{:S(2)}) copy-start(bf16[1024,1024]{1,0:T(8,128)(2,1)} %constant.9.clone.t2_hbm) | copy-start | bytes 6291460
  1.6 1.6 %copy-start.1 = (bf16[1024,1024]{1,0:T(8,128)(2,1)S(1)}, bf16[1024,1024]{1,0:T(8,128)(2,1)}, u32[]{:S(2)}) copy-start(bf16[1024,1024]{1,0:T(8,128)(2,1)} %constant.8.clone.t1_hbm) | copy-start | bytes 6291460
  3.2 0.9 %copy-start.2 = (bf16[16,64,128]{2,1,0:T(8,128)(2,1)S(1)}, bf16[16,64,128]{2,1,0:T(8,128)(2,1)}, u32[]{:S(2)}) copy-start(bf16[16,64,128]{2,1,0:T(8,128)(2,1)} %x_ref.1) | copy-start | bytes 786436
  4.1 0.8 %copy-start.3 = (bf16[2,1,128,128]{3,2,1,0:T(8,128)(2,1)S(1)}, bf16[2,1,128,128]{3,2,1,0:T(8,128)(2,1)}, u32[]{:S(2)}) copy-start(bf16[2,1,128,128]{3,2,1,0:T(8,128)(2,1)} %w1_ref.1) | copy-start | bytes 196612
  5.0 0.8 %copy-start.4 = (bf16[2,1,128,128]{3,2,1,0:T(8,128)(2,1)S(1)}, bf16[2,1,128,128]{3,2,1,0:T(8,128)(2,1)}, u32[]{:S(2)}) copy-start(bf16[2,1,128,128]{3,2,1,0:T(8,128)(2,1)} %w2_ref.1) | copy-start | bytes 196612
  5.8 0.7 copy-start.5
  6.5 0.7 copy-start.6

commit v2 on v1

--- a/solution.py
+++ b/solution.py
@@ -13,44 +13,56 @@
 MESH = pl.DeviceIdType.MESH
 
 
-def tables(total_lat, total_lon):
-    waves = total_lon // 2
-    turn = np.outer(np.arange(waves), np.arange(total_lon)) % total_lon
-    angle = turn * (2.0 * math.pi / total_lon)
-    lon_cos, lon_sin = np.cos(angle), np.sin(angle)
-    lon_forward = np.stack([lon_cos, -lon_sin], axis=1).reshape(2 * waves, total_lon)
-    weight = np.where(np.arange(waves) == 0, 1.0, 2.0)[:, None]
-    lon_inverse = np.stack([weight * lon_cos, -weight * lon_sin], axis=1)
-    lon_inverse = lon_inverse.reshape(2 * waves, total_lon).T
-    turn = np.outer(np.arange(total_lat), np.arange(total_lat)) % total_lat
-    angle = turn * (2.0 * math.pi / total_lat)
-    lat_cos, lat_sin = np.cos(angle), np.sin(angle)
-    lat_forward = np.zeros((2, total_lat, total_lat, 2))
-    lat_forward[0, :, :, 0] = lat_cos
-    lat_forward[0, :, :, 1] = lat_sin
-    lat_forward[1, :, :, 0] = -lat_sin
-    lat_forward[1, :, :, 1] = lat_cos
-    lat_forward = lat_forward.reshape(2 * total_lat, 2 * total_lat)
-    lat_inverse = lat_forward.T
-    return [
-        np.ascontiguousarray(t).astype(jnp.bfloat16)
-        for t in (lon_forward, lat_forward, lat_inverse, lon_inverse)
-    ]
+def wave(turn, length):
+    angle = (turn % length) * (2.0 * math.pi / length)
+    return np.cos(angle), np.sin(angle)
+
+
+def table_bases(total_lat, total_lon):
+    waves = np.arange(total_lon // 2)
+    cells = np.arange(total_lon)
+    lats = np.arange(total_lat)
+    group = np.arange(32)
+    fine = np.arange(16)
+    out = []
+    c, s = wave(16 * np.outer(group, cells), total_lon)
+    pc, ps = wave(np.outer(fine, cells), total_lon)
+    p = np.stack([pc, -ps], axis=1).reshape(32, -1)
+    q = np.stack([-ps, -pc], axis=1).reshape(32, -1)
+    out.append((c, s, p, q))
+    c, s = wave(16 * np.outer(group, np.repeat(lats, 2)), total_lat)
+    pc, ps = wave(np.outer(fine, lats), total_lat)
+    p = np.stack([np.stack([pc, ps], 2), np.stack([-ps, pc], 2)]).reshape(32, -1)
+    q = np.stack([np.stack([-ps, pc], 2), np.stack([-pc, -ps], 2)]).reshape(32, -1)
+    out.append((c, s, p, q))
+    c, s = wave(16 * np.outer(group, np.tile(lats, 2)), total_lat)
+    pc, ps = wave(np.outer(fine, lats), total_lat)
+    p = np.stack([np.stack([pc, -ps], 1), np.stack([ps, pc], 1)], 1).reshape(32, -1)
+    q = np.stack([np.stack([-ps, -pc], 1), np.stack([pc, -ps], 1)], 1).reshape(32, -1)
+    out.append((c, s, p, q))
+    c, s = wave(32 * np.outer(group, np.repeat(waves, 2)), total_lon)
+    pc, ps = wave(np.outer(group, waves), total_lon)
+    p = np.stack([pc, -ps], axis=2).reshape(32, -1)
+    q = np.stack([-ps, -pc], axis=2).reshape(32, -1)
+    out.append((c, s, p, q))
+    return np.stack([np.stack(kind) for kind in out]).astype(np.float32)
 
 
 def mixer_kernel(
     lat_count,
     lon_count,
     x_ref,
-    t1_hbm,
-    t2_hbm,
-    t3_hbm,
-    t4_hbm,
+    bases_hbm,
+    w1_hbm,
+    b1_hbm,
+    w2_hbm,
+    b2_hbm,
+    out_ref,
+    bases,
     w1_ref,
     b1_ref,
     w2_ref,
     b2_ref,
-    out_ref,
     t1,
     t2,
     t3,
@@ -73,12 +85,38 @@
     cells = x_ref.shape[1]
     norm = 1.0 / math.sqrt(lat_count * x_ref.shape[0] * lon_count * cells)
 
-    table_copies = [
-        pltpu.make_async_copy(hbm, vmem, table_sem.at[n])
-        for n, (hbm, vmem) in enumerate(((t1_hbm, t1), (t2_hbm, t2), (t3_hbm, t3), (t4_hbm, t4)))
+    def aligned(index, size):
+        return pl.ds(pl.multiple_of(index * size, size), size)
+
+    fetches = [
+        pltpu.make_async_copy(bases_hbm.at[n], bases.at[n], table_sem.at[n]) for n in range(4)
+    ] + [
+        pltpu.make_async_copy(hbm, vmem, table_sem.at[4 + n])
+        for n, (hbm, vmem) in enumerate(
+            ((w1_hbm, w1_ref), (b1_hbm, b1_ref), (w2_hbm, w2_ref), (b2_hbm, b2_ref))
+        )
     ]
-    for copy in table_copies:
+    for copy in fetches:
         copy.start()
+
+    def build(n, table):
+        fetches[n].wait()
+
+        def group(g, _):
+            c = bases[n, 0, pl.ds(g, 1), :]
+            s = bases[n, 1, pl.ds(g, 1), :]
+            if n == 1:
+                for part in range(2):
+                    near = pl.ds(16 * part, 16)
+                    block = c * bases[n, 2, near, :] + s * bases[n, 3, near, :]
+                    first = pl.multiple_of(table.shape[0] // 2 * part + 16 * g, 16)
+                    table[pl.ds(first, 16), :] = block.astype(table.dtype)
+            else:
+                block = c * bases[n, 2] + s * bases[n, 3]
+                table[aligned(g, 32), :] = block.astype(table.dtype)
+            return 0
+
+        lax.fori_loop(0, 32, group, 0)
 
     barrier = pltpu.get_barrier_semaphore()
 
@@ -117,19 +155,19 @@
     def arrived(stage, landing):
         pltpu.make_async_copy(landing, landing, recv_sem.at[stage]).wait()
 
-    def aligned(index, size):
-        return pl.ds(pl.multiple_of(index * size, size), size)
-
     exchange(0, "lon", lon, lon_count, lambda p: x_ref.at[p], line.at[aligned(lon, cells)])
-    table_copies[0].wait()
+    build(0, t1)
     arrived(0, line)
     spec[...] = jnp.dot(t1[...], line[...], preferred_element_type=jnp.float32).astype(spec.dtype)
 
     exchange(1, "lon", lon, lon_count, lambda p: spec.at[aligned(p, cells)], part.at[lon])
+    build(1, t2)
     arrived(1, part)
 
     exchange(2, "lat", lat, lat_count, lambda p: part.at[:, aligned(p, 2)], column.at[lat])
-    table_copies[1].wait()
+    build(2, t3)
+    for copy in fetches[4:]:
+        copy.wait()
     arrived(2, column)
     height = t2.shape[0] // 2
     spectrum = jnp.dot(
@@ -154,21 +192,21 @@
     act_re = jnp.maximum(hid_re + b1_ref[0], 0.0).astype(jnp.bfloat16)
     act_im = jnp.maximum(hid_im + b1_ref[1], 0.0).astype(jnp.bfloat16)
     out_re, out_im = product(act_re, act_im, w2_ref)
-    mixed[:height] = shrink(out_re + b2_ref[0]).astype(jnp.bfloat16)
-    mixed[height:] = shrink(out_im + b2_ref[1]).astype(jnp.bfloat16)
-    table_copies[2].wait()
+    weight = jnp.where(lat + lon == 0, 0.5, 1.0)
+    mixed[:height] = (shrink(out_re + b2_ref[0]) * weight).astype(jnp.bfloat16)
+    mixed[height:] = (shrink(out_im + b2_ref[1]) * weight).astype(jnp.bfloat16)
     back[...] = jnp.dot(t3[...], mixed[...], preferred_element_type=jnp.float32).astype(back.dtype)
 
     exchange(3, "lat", lat, lat_count, lambda p: back.at[aligned(p, 32)], rows.at[lat])
+    build(3, t4)
     arrived(3, rows)
 
     exchange(4, "lon", lon, lon_count, lambda p: rows.at[:, aligned(p, 2)], waves.at[lon])
-    table_copies[3].wait()
     arrived(4, waves)
     filtered = jnp.dot(
         t4[...], waves.reshape(t4.shape[1], 128)[...], preferred_element_type=jnp.float32
     )
-    field[...] = (filtered * norm).astype(field.dtype)
+    field[...] = (filtered * (2.0 * norm)).astype(field.dtype)
 
     exchange(5, "lon", lon, lon_count, lambda p: field.at[aligned(p, cells)], out_ref.at[lon])
     arrived(5, out_ref)
@@ -185,19 +223,25 @@
     lat_rows, lon_cells, channels = features.shape
     lat_count, lon_count = mesh.shape["lat"], mesh.shape["lon"]
     total_lat, total_lon = lat_rows * lat_count, lon_cells * lon_count
-    consts = [jnp.asarray(t) for t in tables(total_lat, total_lon)]
+    bases = jnp.asarray(table_bases(total_lat, total_lon))
     any_space = pl.BlockSpec(memory_space=pl.ANY)
-    vmem = pl.BlockSpec(memory_space=pltpu.VMEM)
     half = jnp.bfloat16
     waves_own = total_lon // 2 // lon_count
     flat = pltpu.VMEM((total_lon, channels), half)
     filtered = pl.pallas_call(
         functools.partial(mixer_kernel, lat_count, lon_count),
         out_shape=jax.ShapeDtypeStruct((lat_rows, lon_cells, channels), half),
-        in_specs=[any_space] * 5 + [vmem] * 4,
+        in_specs=[any_space] * 6,
         out_specs=any_space,
-        scratch_shapes=[pltpu.VMEM(t.shape, half) for t in consts]
+        scratch_shapes=[
+            pltpu.VMEM(a.shape, a.dtype)
+            for a in (bases, w_first, bias_first, w_second, bias_second)
+        ]
         + [
+            pltpu.VMEM((total_lon, total_lon), half),
+            pltpu.VMEM((2 * total_lat, 2 * total_lat), half),
+            pltpu.VMEM((2 * total_lat, 2 * total_lat), half),
+            pltpu.VMEM((total_lon, total_lon), half),
             flat,
             flat,
             pltpu.VMEM((lon_count, 2 * waves_own, channels), half),
@@ -209,12 +253,12 @@
             flat,
             pltpu.SemaphoreType.DMA((6,)),
             pltpu.SemaphoreType.DMA((6,)),
-            pltpu.SemaphoreType.DMA((4,)),
+            pltpu.SemaphoreType.DMA((8,)),
         ],
         compiler_params=pltpu.CompilerParams(
-            collective_id=0, has_side_effects=True, vmem_limit_bytes=48 * 2**20
+            collective_id=0, has_side_effects=True, vmem_limit_bytes=60 * 2**20
         ),
-    )(features, *consts, w_first, bias_first, w_second, bias_second)
+    )(features, bases, w_first, bias_first, w_second, bias_second)
     return (features.astype(jnp.float32) + filtered.astype(jnp.float32)).astype(features.dtype)
 
 

time: 80.4 us -> 74.3 us (0.924)
  local copies, waits for them, and re-layouts: 7.17 us -> 0.01 us
  other arithmetic: 0.78 us -> 1.73 us
    unnamed x14 -> x2, local copies, waits for them, and re-layouts: 7.17 us -> 0.01 us
    convert_element_type x1, other arithmetic: 0.78 us -> 1.73 us  [body(): (features.astype(jnp.float32) + filtered.astype(jnp.float32)).astype(feat...]
where the time goes in v2:
time: 74.3 us; the launch traced here: 74.1 us
  Pallas kernels  72.4 us (97%)
  other arithmetic  1.73 us (2%)
    pallas_call x1, Pallas kernels, body(): pl.pallas_call(functools.partial(mixer_kernel, lat_count, lon_count), out...  72.4 us
    convert_element_type x1, other arithmetic, body(): (features.astype(jnp.float32) + filtered.astype(jnp.float32)).astype(feat...  1.73 us

profile of v2, /device:TPU:1, one launch (start us, length us, event | category | flops | bytes accessed | tf_op | source)
XLA Modules:
  0.0 74.1 jit_solution(6473846147747965655)
XLA Ops:
  0.0 0.0 copy-start
  0.0 72.4 %shard_map.64 = bf16[16,64,128]{2,1,0:T(8,128)(2,1)} custom-call(bf16[16,64,128]{2,1,0:T(8,128)(2,1)} %x_ref.1, f32[4,4,32,1024]{3,2,1,0:T(8,128)} %constant.2.clone.bases_hbm, bf16[2,1,128,128]{3,2,1,0:T(8,128)(2,1)} %w1_hbm.1, f32[2,1,128]{2,1,0:T(1,128)} %b1_hbm.1, bf16[2,1,128,128]{3,2,1,0:T(8,128)(2,1)} %w2_hbm.1, f32[2,1,128]{2,1,0:T(1,128)} %b2_hbm.1), custom_call_target="tpu_custom_call" | custom-call | tf_op jit(solution)/shard_map/pallas_call | solution.py:231
  72.4 0.0 copy-done
  72.4 1.7 %add_convert_fusion = bf16[16,64,128]{2,1,0:T(8,128)(2,1)} fusion(bf16[16,64,128]{2,1,0:T(8,128)(2,1)} %shard_map.64, bf16[16,64,128]{2,1,0:T(8,128)(2,1)S(1)} %copy-done), kind=kLoop, calls=%fused_computation | loop fusion | flops 524288 | bytes 786432 | tf_op jit(solution)/shard_map/convert_element_type | solution.py:262
Async XLA Ops:
  0.0 72.4 %copy-start = (bf16[16,64,128]{2,1,0:T(8,128)(2,1)S(1)}, bf16[16,64,128]{2,1,0:T(8,128)(2,1)}, u32[]{:S(2)}) copy-start(bf16[16,64,128]{2,1,0:T(8,128)(2,1)} %x_ref.1) | copy-start | bytes 786436

commit v3 on v2

v3 whole, which is shorter than its diff:
```python
import functools
import math

import jax
import jax.numpy as jnp
import numpy as np
from jax import lax
from jax.experimental import pallas as pl
from jax.experimental.pallas import tpu as pltpu
from jax.sharding import PartitionSpec as P

shrink_level = 0.01
MESH = pl.DeviceIdType.MESH


def wave(turn, length):
    angle = (turn % length) * (2.0 * math.pi / length)
    return np.cos(angle), np.sin(angle)


def table_bases(total_lat, total_lon):
    waves = np.arange(total_lon // 2)
    cells = np.arange(total_lon)
    lats = np.arange(total_lat)
    group = np.arange(32)
    fine = np.arange(16)
    out = []
    c, s = wave(16 * np.outer(group, cells), total_lon)
    pc, ps = wave(np.outer(fine, cells), total_lon)
    p = np.stack([pc, -ps], axis=1).reshape(32, -1)
    q = np.stack([-ps, -pc], axis=1).reshape(32, -1)
    out.append((c, s, p, q))
    c, s = wave(16 * np.outer(group, np.repeat(lats, 2)), total_lat)
    pc, ps = wave(np.outer(fine, lats), total_lat)
    p = np.stack([np.stack([pc, ps], 2), np.stack([-ps, pc], 2)]).reshape(32, -1)
    q = np.stack([np.stack([-ps, pc], 2), np.stack([-pc, -ps], 2)]).reshape(32, -1)
    out.append((c, s, p, q))
    c, s = wave(16 * np.outer(group, np.tile(lats, 2)), total_lat)
    pc, ps = wave(np.outer(fine, lats), total_lat)
    p = np.stack([np.stack([pc, -ps], 1), np.stack([ps, pc], 1)], 1).reshape(32, -1)
    q = np.stack([np.stack([-ps, -pc], 1), np.stack([pc, -ps], 1)], 1).reshape(32, -1)
    out.append((c, s, p, q))
    c, s = wave(32 * np.outer(group, np.repeat(waves, 2)), total_lon)
    pc, ps = wave(np.outer(group, waves), total_lon)
    p = np.stack([pc, -ps], axis=2).reshape(32, -1)
    q = np.stack([-ps, -pc], axis=2).reshape(32, -1)
    out.append((c, s, p, q))
    return np.stack([np.stack(kind) for kind in out]).astype(np.float32)


def aligned(index, size):
    return pl.ds(pl.multiple_of(index * size, size), size)


def far_first(step):
    half = (step + 1) // 2
    return lax.rem(4 + half - 2 * half * lax.rem(step, 2) + 8, 8)


def mixer_kernel(
    x_ref,
    bases_hbm,
    w1_hbm,
    b1_hbm,
    w2_hbm,
    b2_hbm,
    landed,
    bases,
    w1_ref,
    b1_ref,
    w2_ref,
    b2_ref,
    t1,
    t2,
    t3,
    t4,
    swap,
    line,
    spec,
    part,
    by_wave,
    column,
    mixed,
    back,
    rows,
    by_row,
    waves,
    field,
    send_sem,
    recv_sem,
    table_sem,
):
    lat = lax.axis_index("lat")
    lon = lax.axis_index("lon")
    x_hi, y, core = lat // 16, lax.rem(lat // 2, 8), lax.rem(lat, 2)
    z, x_lo = lon // 2, lax.rem(lon, 2)
    z_hi = lon // 8
    norm = 1.0 / math.sqrt(t2.shape[0] // 2 * t1.shape[1])

    fetches = [
        pltpu.make_async_copy(bases_hbm.at[n], bases.at[n], table_sem.at[n]) for n in range(4)
    ] + [
        pltpu.make_async_copy(hbm, vmem, table_sem.at[4 + n])
        for n, (hbm, vmem) in enumerate(
            ((w1_hbm, w1_ref), (b1_hbm, b1_ref), (w2_hbm, w2_ref), (b2_hbm, b2_ref))
        )
    ]
    for copy in fetches:
        copy.start()

    def build(n, table):
        fetches[n].wait()
        first = (1 - x_hi) if n == 0 else (1 - z_hi)

        def group(g, _):
            c = bases[n, 0, pl.ds(g, 1), :]
            s = bases[n, 1, pl.ds(g, 1), :]
            if n in (1, 2):
                for half in range(2):
                    near = pl.ds(16 * half, 16)
                    block = c * bases[n, 2, near, :] + s * bases[n, 3, near, :]
                    turn = half if n == 1 else lax.rem(half + first, 2)
                    start = pl.multiple_of(512 * turn + 16 * g, 16)
                    table[pl.ds(start, 16), :] = block.astype(table.dtype)
            else:
                block = c * bases[n, 2] + s * bases[n, 3]
                start = 32 * g if n == 3 else 512 * lax.rem(g + first, 2) + 32 * (g // 2)
                table[pl.ds(pl.multiple_of(start, 32), 32), :] = block.astype(table.dtype)
            return 0

        lax.fori_loop(0, 32, group, 0)

    barrier = pltpu.get_barrier_semaphore()

    def greet_lon(step, _):
        peer = lax.rem(lon + step, 16)
        pl.semaphore_signal(barrier, inc=1, device_id={"lon": peer}, device_id_type=MESH)
        return 0

    def greet_lat(step, _):
        peer = lax.rem(lat + step, 32)
        pl.semaphore_signal(barrier, inc=1, device_id={"lat": peer}, device_id_type=MESH)
        return 0

    lax.fori_loop(1, 16, greet_lon, 0)
    lax.fori_loop(1, 32, greet_lat, 0)
    pl.semaphore_wait(barrier, 46)

    def lon_peer(step):
        return lax.rem(z + far_first(step // 2), 8) * 2 + lax.rem(x_lo + 1 + step, 2)

    def lat_peer(other, step):
        place = lax.rem(y + far_first(step // 2), 8) * 2 + lax.rem(core + 1 + step, 2)
        return lax.rem(x_hi + other, 2) * 16 + place

    def push(slot, axis, steps, peer_of, source, target):
        def send(step, _):
            peer = peer_of(step)
            pltpu.make_async_remote_copy(
                src_ref=source(peer),
                dst_ref=target,
                send_sem=send_sem.at[slot],
                recv_sem=recv_sem.at[slot],
                device_id={axis: peer},
                device_id_type=MESH,
            ).start()
            return 0

        lax.fori_loop(steps[0], steps[1], send, 0)

    def keep(slot, source, target):
        pltpu.make_async_copy(source, target, recv_sem.at[slot]).start()

    def arrived(slot, landing):
        pltpu.make_async_copy(landing, landing, recv_sem.at[slot]).wait()

    def regroup(block):
        flat = block.reshape(256, block.shape[-1])
        return jnp.dot(swap[...], flat, preferred_element_type=jnp.float32).astype(flat.dtype)

    keep(0, x_ref.at[lon], line.at[aligned(lon, 64)])
    push(0, "lon", (0, 15), lon_peer, lambda p: x_ref.at[p], line.at[aligned(lon, 64)])
    build(0, t1)
    row = lax.broadcasted_iota(jnp.int32, swap.shape, 0)
    col = lax.broadcasted_iota(jnp.int32, swap.shape, 1)
    source = (row % 32) // 2 * 16 + row // 32 * 2 + row % 2
    swap[...] = jnp.where(col == source, 1.0, 0.0).astype(swap.dtype)
    arrived(0, line)

    for turn in range(2):
        height = pl.ds(512 * turn, 512)
        spec[height, :] = jnp.dot(
            t1[height, :], line[...], preferred_element_type=jnp.float32
        ).astype(spec.dtype)
        keep(1 + turn, spec.at[pl.ds(pl.multiple_of(512 * turn + 32 * lon, 32), 32)], part.at[turn, lon])
        push(
            1 + turn,
            "lon",
            (0, 15),
            lon_peer,
            lambda p, turn=turn: spec.at[pl.ds(pl.multiple_of(512 * turn + 32 * p, 32), 32)],
            part.at[turn, lon],
        )
    build(1, t2)

    for turn in range(2):
        arrived(1 + turn, part.at[turn])
        for eight in range(2):
            block = regroup(part[turn, :, 16 * eight : 16 * eight + 16, :])
            by_wave[turn, 8 * eight : 8 * eight + 8] = block.reshape(8, 32, block.shape[-1])
        if turn == 1:
            keep(3, by_wave.at[turn, lax.rem(lat, 16)], column.at[aligned(lat, 32)])
        push(
            3,
            "lat",
            (0, 16 - turn),
            functools.partial(lat_peer, 1 - turn),
            lambda p, turn=turn: by_wave.at[turn, lax.rem(p, 16)],
            column.at[aligned(lat, 32)],
        )
    build(2, t3)
    for copy in fetches[4:]:
        copy.wait()
    arrived(3, column)
    spectrum = jnp.dot(t2[...], column[...], preferred_element_type=jnp.float32)
    spectrum = (spectrum * norm).astype(jnp.bfloat16)

    def product(left_re, left_im, w_ref):
        w_re, w_im = w_ref[0, 0], w_ref[1, 0]
        re = jnp.dot(left_re, w_re, preferred_element_type=jnp.float32) - jnp.dot(
            left_im, w_im, preferred_element_type=jnp.float32
        )
        im = jnp.dot(left_im, w_re, preferred_element_type=jnp.float32) + jnp.dot(
            left_re, w_im, preferred_element_type=jnp.float32
        )
        return re, im

    def shrink(v):
        return jnp.maximum(v - shrink_level, 0.0) + jnp.minimum(v + shrink_level, 0.0)

    hid_re, hid_im = product(spectrum[:512], spectrum[512:], w1_ref)
    act_re = jnp.maximum(hid_re + b1_ref[0], 0.0).astype(jnp.bfloat16)
    act_im = jnp.maximum(hid_im + b1_ref[1], 0.0).astype(jnp.bfloat16)
    out_re, out_im = product(act_re, act_im, w2_ref)
    weight = jnp.where(lat + lon == 0, 0.5, 1.0)
    mixed[:512] = (shrink(out_re + b2_ref[0]) * weight).astype(jnp.bfloat16)
    mixed[512:] = (shrink(out_im + b2_ref[1]) * weight).astype(jnp.bfloat16)

    for turn in range(2):
        height = pl.ds(512 * turn, 512)
        back[height, :] = jnp.dot(
            t3[height, :], mixed[...], preferred_element_type=jnp.float32
        ).astype(back.dtype)
        keep(4 + turn, back.at[pl.ds(pl.multiple_of(512 * turn + 16 * lat, 16), 16)], rows.at[turn, lat])
        for near in range(2):
            push(
                4 + turn,
                "lat",
                (0, 16 - near),
                functools.partial(lat_peer, 1 - near),
                lambda p, turn=turn: back.at[pl.ds(pl.multiple_of(512 * turn + 16 * p, 16), 16)],
                rows.at[turn, lat],
            )
    build(3, t4)

    for turn in range(2):
        arrived(4 + turn, rows.at[turn])
        for half in range(2):
            block = regroup(rows[turn, 16 * half : 16 * half + 16])
            by_row[turn, :, 32 * half : 32 * half + 32, :] = block.reshape(8, 32, block.shape[-1])
        if turn == 1:
            keep(6, by_row.at[turn, lax.rem(lon, 8)], waves.at[aligned(lon, 64)])
        push(
            6,
            "lon",
            (turn, 8),
            lambda step, turn=turn: lax.rem(z_hi + 1 - turn, 2) * 8 + lax.rem(lon + step, 8),
            lambda p, turn=turn: by_row.at[turn, lax.rem(p, 8)],
            waves.at[aligned(lon, 64)],
        )
    arrived(6, waves)
    filtered = jnp.dot(t4[...], waves[...], preferred_element_type=jnp.float32)
    field[...] = (filtered * (2.0 * norm)).astype(field.dtype)

    keep(7, field.at[aligned(lon, 64)], landed.at[lon])
    push(7, "lon", (0, 15), lon_peer, lambda p: field.at[aligned(p, 64)], landed.at[lon])
    arrived(7, landed)

    for slot, sent in enumerate((960, 480, 480, 992, 496, 496, 960, 960)):
        left = line.at[pl.ds(0, sent)]
        pltpu.make_async_copy(left, left, send_sem.at[slot]).wait()


def body(features, w_first, bias_first, w_second, bias_second):
    lat_rows, lon_cells, channels = features.shape
    lat_count, lon_count = lax.axis_size("lat"), lax.axis_size("lon")
    total_lat, total_lon = lat_rows * lat_count, lon_cells * lon_count
    bases = jnp.asarray(table_bases(total_lat, total_lon))
    hbm = pl.BlockSpec(memory_space=pltpu.HBM)
    half = jnp.bfloat16
    flat = pltpu.VMEM((1024, channels), half)
    table = pltpu.VMEM((1024, 1024), half)
    filtered = pl.pallas_call(
        mixer_kernel,
        out_shape=jax.ShapeDtypeStruct((lat_rows, lon_cells, channels), half),
        in_specs=[hbm] * 6,
        out_specs=pl.BlockSpec(memory_space=pltpu.VMEM),
        scratch_shapes=[
            pltpu.VMEM(a.shape, a.dtype)
            for a in (bases, w_first, bias_first, w_second, bias_second)
        ]
        + [table] * 4
        + [
            pltpu.VMEM((256, 256), half),
            flat,
            flat,
            pltpu.VMEM((2, 16, 32, channels), half),
            pltpu.VMEM((2, 16, 32, channels), half),
            flat,
            flat,
            flat,
            pltpu.VMEM((2, 32, 16, channels), half),
            pltpu.VMEM((2, 8, 64, channels), half),
            flat,
            flat,
            pltpu.SemaphoreType.DMA((8,)),
            pltpu.SemaphoreType.DMA((8,)),
            pltpu.SemaphoreType.DMA((8,)),
        ],
        compiler_params=pltpu.CompilerParams(
            collective_id=0, has_side_effects=True, vmem_limit_bytes=40 * 2**20
        ),
    )(
        *(
            pltpu.with_memory_space_constraint(a, pltpu.HBM)
            for a in (features, bases, w_first, bias_first, w_second, bias_second)
        )
    )
    return (features.astype(jnp.float32) + filtered.astype(jnp.float32)).astype(features.dtype)


def solution(mesh):
    in_specs = (P("lat", "lon", None), P(), P(), P(), P())
    out_specs = P("lat", "lon", None)
    return jax.shard_map(
        body, mesh=mesh, in_specs=in_specs, out_specs=out_specs, check_vma=False
    )
```

time: 74.3 us -> 67.3 us (0.906)
  Pallas kernels: 72.4 us -> 66.4 us
  other arithmetic: 1.73 us -> 0.78 us
    pallas_call x1, Pallas kernels: 72.4 us -> 66.4 us  [body(): pl.pallas_call(mixer_kernel, out_shape=jax.ShapeDtypeStruct((lat_rows, lo...]
    convert_element_type x1, other arithmetic: 1.73 us -> 0.78 us  [body(): (features.astype(jnp.float32) + filtered.astype(jnp.float32)).astype(feat...]
where the time goes in v3:
time: 67.3 us; the launch traced here: 67.2 us
  Pallas kernels  66.4 us (99%)
  other arithmetic  0.78 us (1%)
    pallas_call x1, Pallas kernels, body(): pl.pallas_call(mixer_kernel, out_shape=jax.ShapeDtypeStruct((lat_rows, lo...  66.4 us

profile of v3, /device:TPU:1, one launch (start us, length us, event | category | flops | bytes accessed | tf_op | source)
XLA Modules:
  0.0 67.2 jit_solution(3788865683094245025)
XLA Ops:
  0.0 0.0 copy-start
  0.0 66.4 %shard_map.64 = bf16[16,64,128]{2,1,0:T(8,128)(2,1)S(1)} custom-call(bf16[16,64,128]{2,1,0:T(8,128)(2,1)} %x_ref.1, f32[4,4,32,1024]{3,2,1,0:T(8,128)} %constant.2.clone.bases_hbm, bf16[2,1,128,128]{3,2,1,0:T(8,128)(2,1)} %w1_hbm.1, f32[2,1,128]{2,1,0:T(1,128)} %b1_hbm.1, bf16[2,1,128,128]{3,2,1,0:T(8,128)(2,1)} %w2_hbm.1, f32[2,1,128]{2,1,0:T(1,128)} %b2_hbm.1), custom_call_target="tpu_custom_call" | custom-call | tf_op jit(solution)/shard_map/pallas_call | solution.py:303
  66.4 0.0 copy-done
  66.4 0.8 %add_convert_fusion = bf16[16,64,128]{2,1,0:T(8,128)(2,1)} fusion(bf16[16,64,128]{2,1,0:T(8,128)(2,1)S(1)} %shard_map.64, bf16[16,64,128]{2,1,0:T(8,128)(2,1)S(1)} %copy-done), kind=kLoop, calls=%fused_computation | loop fusion | flops 524288 | bytes 786432 | tf_op jit(solution)/shard_map/convert_element_type | solution.py:339
Async XLA Ops:
  0.0 66.4 %copy-start = (bf16[16,64,128]{2,1,0:T(8,128)(2,1)S(1)}, bf16[16,64,128]{2,1,0:T(8,128)(2,1)}, u32[]{:S(2)}) copy-start(bf16[16,64,128]{2,1,0:T(8,128)(2,1)} %x_ref.1) | copy-start | bytes 786436

commit v4 on v3

v4 whole, which is shorter than its diff:
```python
import functools
import math

import jax
import jax.numpy as jnp
import numpy as np
from jax import lax
from jax.experimental import pallas as pl
from jax.experimental.pallas import tpu as pltpu
from jax.sharding import PartitionSpec as P

shrink_level = 0.01
MESH = pl.DeviceIdType.MESH


def wave(turn, length):
    angle = (turn % length) * (2.0 * math.pi / length)
    return np.cos(angle), np.sin(angle)


def table_bases(total_lat, total_lon):
    waves = np.arange(total_lon // 2)
    cells = np.arange(total_lon)
    lats = np.arange(total_lat)
    group = np.arange(32)
    fine = np.arange(16)
    place, core = lats // 2, lats % 2
    row_y, row_z, row_hi, row_lo = place // 32, place // 4 % 8, place // 2 % 2, place % 2
    row = 16 * ((row_hi * 8 + row_y) * 2 + core) + 2 * row_z + row_lo
    out = []
    c, s = wave(16 * np.outer(group, cells), total_lon)
    pc, ps = wave(np.outer(fine, cells), total_lon)
    p = np.stack([pc, -ps], axis=1).reshape(32, -1)
    q = np.stack([-ps, -pc], axis=1).reshape(32, -1)
    out.append((c, s, p, q))
    c, s = wave(16 * np.outer(group, np.repeat(row, 2)), total_lat)
    pc, ps = wave(np.outer(fine, row), total_lat)
    p = np.stack([np.stack([pc, ps], 2), np.stack([-ps, pc], 2)]).reshape(32, -1)
    q = np.stack([np.stack([-ps, pc], 2), np.stack([-pc, -ps], 2)]).reshape(32, -1)
    out.append((c, s, p, q))
    c, s = wave(np.outer(row[::16], np.tile(lats, 2)), total_lat)
    pc, ps = wave(np.outer(row[:16], lats), total_lat)
    p = np.stack([np.stack([pc, -ps], 1), np.stack([ps, pc], 1)], 1).reshape(32, -1)
    q = np.stack([np.stack([-ps, -pc], 1), np.stack([pc, -ps], 1)], 1).reshape(32, -1)
    out.append((c, s, p, q))
    c, s = wave(32 * np.outer(group, np.repeat(waves, 2)), total_lon)
    pc, ps = wave(np.outer(group, waves), total_lon)
    p = np.stack([pc, -ps], axis=2).reshape(32, -1)
    q = np.stack([-ps, -pc], axis=2).reshape(32, -1)
    out.append((c, s, p, q))
    return np.stack([np.stack(kind) for kind in out]).astype(np.float32)


def wide_order():
    def hops(o):
        return min(o[0], 8 - o[0]) + min(o[1], 8 - o[1]) + 2 * o[2] + o[3]

    offsets = [(y, z, h, l) for y in range(8) for z in range(8) for h in range(2) for l in range(2)]
    return sorted(offsets[1:], key=lambda o: -hops(o))


def aligned(index, size):
    return pl.ds(pl.multiple_of(index * size, size), size)


def far_first(step):
    half = (step + 1) // 2
    return lax.rem(4 + half - 2 * half * lax.rem(step, 2) + 8, 8)


def mixer_kernel(
    x_ref,
    bases_hbm,
    w1_hbm,
    b1_hbm,
    w2_hbm,
    b2_hbm,
    landed,
    bases,
    w1_ref,
    b1_ref,
    w2_ref,
    b2_ref,
    t1,
    t2,
    t3,
    t4,
    swap,
    swap_back,
    line,
    spec,
    pair,
    by_place,
    column,
    mixed,
    back,
    wide,
    pair_back,
    waves,
    field,
    send_sem,
    recv_sem,
    table_sem,
):
    lat = lax.axis_index("lat")
    lon = lax.axis_index("lon")
    x_hi, y, core = lat // 16, lax.rem(lat // 2, 8), lax.rem(lat, 2)
    z, x_lo = lon // 2, lax.rem(lon, 2)
    z_hi = lon // 8
    norm = 1.0 / math.sqrt(t2.shape[0] // 2 * t1.shape[1])

    fetches = [
        pltpu.make_async_copy(bases_hbm.at[n], bases.at[n], table_sem.at[n]) for n in range(4)
    ] + [
        pltpu.make_async_copy(hbm, vmem, table_sem.at[4 + n])
        for n, (hbm, vmem) in enumerate(
            ((w1_hbm, w1_ref), (b1_hbm, b1_ref), (w2_hbm, w2_ref), (b2_hbm, b2_ref))
        )
    ]
    for copy in fetches:
        copy.start()

    def build(n, table):
        fetches[n].wait()

        def group(g, _):
            c = bases[n, 0, pl.ds(g, 1), :]
            s = bases[n, 1, pl.ds(g, 1), :]
            if n == 1:
                for part in range(2):
                    near = pl.ds(16 * part, 16)
                    block = c * bases[n, 2, near, :] + s * bases[n, 3, near, :]
                    start = pl.multiple_of(512 * part + 16 * g, 16)
                    table[pl.ds(start, 16), :] = block.astype(table.dtype)
            else:
                table[aligned(g, 32), :] = (c * bases[n, 2] + s * bases[n, 3]).astype(table.dtype)
            return 0

        lax.fori_loop(0, 32, group, 0)

    barrier = pltpu.get_barrier_semaphore()

    def greet_lon(step, _):
        peer = lax.rem(lon + step, 16)
        pl.semaphore_signal(barrier, inc=1, device_id={"lon": peer}, device_id_type=MESH)
        return 0

    def greet_lat(step, _):
        peer = lax.rem(lat + 2 * step, 32)
        pl.semaphore_signal(barrier, inc=1, device_id={"lat": peer}, device_id_type=MESH)
        return 0

    sibling = lat + 1 - 2 * core
    lax.fori_loop(1, 16, greet_lon, 0)
    lax.fori_loop(1, 16, greet_lat, 0)
    pl.semaphore_signal(barrier, inc=1, device_id={"lat": sibling}, device_id_type=MESH)
    pl.semaphore_wait(barrier, 31)

    def lon_peer(step):
        return lax.rem(z + far_first(step // 2), 8) * 2 + lax.rem(x_lo + 1 + step, 2)

    def push(slot, axis, steps, peer_of, source, target):
        def send(step, _):
            peer = peer_of(step)
            pltpu.make_async_remote_copy(
                src_ref=source(peer),
                dst_ref=target,
                send_sem=send_sem.at[slot],
                recv_sem=recv_sem.at[slot],
                device_id={axis: peer},
                device_id_type=MESH,
            ).start()
            return 0

        lax.fori_loop(steps[0], steps[1], send, 0)

    def keep(slot, source, target):
        pltpu.make_async_copy(source, target, recv_sem.at[slot]).start()

    def arrived(slot, landing):
        pltpu.make_async_copy(landing, landing, recv_sem.at[slot]).wait()

    def to_sibling(slot, source, target):
        pltpu.make_async_remote_copy(
            src_ref=source,
            dst_ref=target,
            send_sem=send_sem.at[slot],
            recv_sem=recv_sem.at[slot],
            device_id={"lat": sibling},
            device_id_type=MESH,
        ).start()

    ys = [lax.rem(y + step, 8) for step in range(8)]
    zs = [lax.rem(z + step, 8) for step in range(8)]
    his = [x_hi, 1 - x_hi]
    los = [x_lo, 1 - x_lo]
    place = ((y * 8 + z) * 2 + x_hi) * 2 + x_lo

    def to_chips(slot, source, landing):
        keep(slot, source.at[aligned(place, 4)], landing.at[aligned(place, 4)])
        for dy, dz, dh, dl in wide_order():
            other = ((ys[dy] * 8 + zs[dz]) * 2 + his[dh]) * 2 + los[dl]
            pltpu.make_async_remote_copy(
                src_ref=source.at[aligned(other, 4)],
                dst_ref=landing.at[aligned(place, 4)],
                send_sem=send_sem.at[slot],
                recv_sem=recv_sem.at[slot],
                device_id={
                    "lat": (his[dh] * 8 + ys[dy]) * 2 + core,
                    "lon": zs[dz] * 2 + los[dl],
                },
                device_id_type=MESH,
            ).start()

    keep(0, x_ref.at[lon], line.at[aligned(lon, 64)])
    push(0, "lon", (0, 15), lon_peer, lambda p: x_ref.at[p], line.at[aligned(lon, 64)])
    build(0, t1)
    row = lax.broadcasted_iota(jnp.int32, swap.shape, 0)
    col = lax.broadcasted_iota(jnp.int32, swap.shape, 1)
    source = row // 2 % 2 * 128 + row // 4 * 2 + row % 2
    swap[...] = jnp.where(col == source, 1.0, 0.0).astype(swap.dtype)
    source = col // 2 % 2 * 128 + col // 4 * 2 + col % 2
    swap_back[...] = jnp.where(row == source, 1.0, 0.0).astype(swap.dtype)
    arrived(0, line)

    def half_of(which):
        rows = pl.ds(pl.multiple_of(512 * which, 512), 512)
        return jnp.dot(t1[rows, :], line[...], preferred_element_type=jnp.float32).astype(spec.dtype)

    spec[...] = half_of(1 - core)
    to_sibling(1, spec, pair.at[core])
    pair[core] = half_of(core)
    arrived(1, spec)

    for block in range(4):
        both = pair[:, 128 * block : 128 * block + 128, :].reshape(256, -1)
        both = jnp.dot(swap[...], both, preferred_element_type=jnp.float32)
        by_place[256 * block : 256 * block + 256, :] = both.astype(by_place.dtype)
    to_chips(2, by_place, column)
    build(1, t2)
    build(2, t3)
    for copy in fetches[4:]:
        copy.wait()
    arrived(2, column)
    spectrum = jnp.dot(t2[...], column[...], preferred_element_type=jnp.float32)
    spectrum = (spectrum * norm).astype(jnp.bfloat16)

    def product(left_re, left_im, w_ref):
        w_re, w_im = w_ref[0, 0], w_ref[1, 0]
        re = jnp.dot(left_re, w_re, preferred_element_type=jnp.float32) - jnp.dot(
            left_im, w_im, preferred_element_type=jnp.float32
        )
        im = jnp.dot(left_im, w_re, preferred_element_type=jnp.float32) + jnp.dot(
            left_re, w_im, preferred_element_type=jnp.float32
        )
        return re, im

    def shrink(v):
        return jnp.maximum(v - shrink_level, 0.0) + jnp.minimum(v + shrink_level, 0.0)

    hid_re, hid_im = product(spectrum[:512], spectrum[512:], w1_ref)
    act_re = jnp.maximum(hid_re + b1_ref[0], 0.0).astype(jnp.bfloat16)
    act_im = jnp.maximum(hid_im + b1_ref[1], 0.0).astype(jnp.bfloat16)
    out_re, out_im = product(act_re, act_im, w2_ref)
    weight = jnp.where(lat + lon == 0, 0.5, 1.0)
    mixed[:512] = (shrink(out_re + b2_ref[0]) * weight).astype(jnp.bfloat16)
    mixed[512:] = (shrink(out_im + b2_ref[1]) * weight).astype(jnp.bfloat16)

    back[...] = jnp.dot(t3[...], mixed[...], preferred_element_type=jnp.float32).astype(back.dtype)
    to_chips(3, back, wide)
    build(3, t4)
    arrived(3, wide)

    for block in range(4):
        both = wide[256 * block : 256 * block + 256, :]
        both = jnp.dot(swap_back[...], both, preferred_element_type=jnp.float32)
        both = both.astype(wide.dtype).reshape(2, 128, -1)
        pair_back[:, 128 * block : 128 * block + 128, :] = both
    to_sibling(4, pair_back.at[1 - core], waves)

    def part_of(half, which, operand):
        rows = pl.ds(pl.multiple_of(512 * half, 512), 512)
        columns = pl.ds(pl.multiple_of(512 * which, 512), 512)
        return jnp.dot(t4[rows, columns], operand, preferred_element_type=jnp.float32)

    far = 1 - z_hi
    held = [part_of(half, core, pair_back[core]) for half in (far, z_hi)]
    arrived(4, waves)
    for turn, half in enumerate((far, z_hi)):
        filtered = held[turn] + part_of(half, 1 - core, waves[...])
        field[512 * turn : 512 * turn + 512, :] = (filtered * (2.0 * norm)).astype(field.dtype)

        def block_of(peer, turn=turn):
            return field.at[pl.ds(pl.multiple_of(512 * turn + 64 * lax.rem(peer, 8), 64), 64)]

        if turn == 1:
            keep(5, block_of(lon), landed.at[lon])
        push(
            5,
            "lon",
            (turn, 8),
            lambda step, half=half: half * 8 + lax.rem(lon + step, 8),
            block_of,
            landed.at[lon],
        )
    arrived(5, landed)

    for slot, sent in enumerate((960, 512, 1020, 1020, 512, 960)):
        left = line.at[pl.ds(0, sent)]
        pltpu.make_async_copy(left, left, send_sem.at[slot]).wait()


def body(features, w_first, bias_first, w_second, bias_second):
    lat_rows, lon_cells, channels = features.shape
    lat_count, lon_count = lax.axis_size("lat"), lax.axis_size("lon")
    total_lat, total_lon = lat_rows * lat_count, lon_cells * lon_count
    bases = jnp.asarray(table_bases(total_lat, total_lon))
    hbm = pl.BlockSpec(memory_space=pltpu.HBM)
    half = jnp.bfloat16
    flat = pltpu.VMEM((1024, channels), half)
    table = pltpu.VMEM((1024, 1024), half)
    filtered = pl.pallas_call(
        mixer_kernel,
        out_shape=jax.ShapeDtypeStruct((lat_rows, lon_cells, channels), half),
        in_specs=[hbm] * 6,
        out_specs=pl.BlockSpec(memory_space=pltpu.VMEM),
        scratch_shapes=[
            pltpu.VMEM(a.shape, a.dtype)
            for a in (bases, w_first, bias_first, w_second, bias_second)
        ]
        + [table] * 4
        + [
            pltpu.VMEM((256, 256), half),
            pltpu.VMEM((256, 256), half),
            flat,
            pltpu.VMEM((512, channels), half),
            pltpu.VMEM((2, 512, channels), half),
            flat,
            flat,
            flat,
            flat,
            flat,
            pltpu.VMEM((2, 512, channels), half),
            pltpu.VMEM((512, channels), half),
            flat,
            pltpu.SemaphoreType.DMA((6,)),
            pltpu.SemaphoreType.DMA((6,)),
            pltpu.SemaphoreType.DMA((8,)),
        ],
        compiler_params=pltpu.CompilerParams(
            collective_id=0, has_side_effects=True, vmem_limit_bytes=40 * 2**20
        ),
    )(
        *(
            pltpu.with_memory_space_constraint(a, pltpu.HBM)
            for a in (features, bases, w_first, bias_first, w_second, bias_second)
        )
    )
    return (features.astype(jnp.float32) + filtered.astype(jnp.float32)).astype(features.dtype)


def solution(mesh):
    in_specs = (P("lat", "lon", None), P(), P(), P(), P())
    out_specs = P("lat", "lon", None)
    return jax.shard_map(
        body, mesh=mesh, in_specs=in_specs, out_specs=out_specs, check_vma=False
    )
```

time: 67.3 us -> 61.5 us (0.914)
  Pallas kernels: 66.4 us -> 60.6 us
    pallas_call x1, Pallas kernels: 66.4 us -> 60.6 us  [body(): pl.pallas_call(mixer_kernel, out_shape=jax.ShapeDtypeStruct((lat_rows, lo...]
where the time goes in v4:
time: 61.5 us; the launch traced here: 61.4 us
  Pallas kernels  60.6 us (99%)
  other arithmetic  0.78 us (1%)
    pallas_call x1, Pallas kernels, body(): pl.pallas_call(mixer_kernel, out_shape=jax.ShapeDtypeStruct((lat_rows, lo...  60.6 us

profile of v4, /device:TPU:1, one launch (start us, length us, event | category | flops | bytes accessed | tf_op | source)
XLA Modules:
  0.0 61.4 jit_solution(473208974855617877)
XLA Ops:
  0.0 0.0 copy-start
  0.0 60.6 %shard_map.64 = bf16[16,64,128]{2,1,0:T(8,128)(2,1)S(1)} custom-call(bf16[16,64,128]{2,1,0:T(8,128)(2,1)} %x_ref.1, f32[4,4,32,1024]{3,2,1,0:T(8,128)} %constant.2.clone.bases_hbm, bf16[2,1,128,128]{3,2,1,0:T(8,128)(2,1)} %w1_hbm.1, f32[2,1,128]{2,1,0:T(1,128)} %b1_hbm.1, bf16[2,1,128,128]{3,2,1,0:T(8,128)(2,1)} %w2_hbm.1, f32[2,1,128]{2,1,0:T(1,128)} %b2_hbm.1), custom_call_target="tpu_custom_call" | custom-call | tf_op jit(solution)/shard_map/pallas_call | solution.py:322
  60.7 0.0 copy-done
  60.7 0.8 %add_convert_fusion = bf16[16,64,128]{2,1,0:T(8,128)(2,1)} fusion(bf16[16,64,128]{2,1,0:T(8,128)(2,1)S(1)} %shard_map.64, bf16[16,64,128]{2,1,0:T(8,128)(2,1)S(1)} %copy-done), kind=kLoop, calls=%fused_computation | loop fusion | flops 524288 | bytes 786432 | tf_op jit(solution)/shard_map/convert_element_type | solution.py:359
Async XLA Ops:
  0.0 60.7 %copy-start = (bf16[16,64,128]{2,1,0:T(8,128)(2,1)S(1)}, bf16[16,64,128]{2,1,0:T(8,128)(2,1)}, u32[]{:S(2)}) copy-start(bf16[16,64,128]{2,1,0:T(8,128)(2,1)} %x_ref.1) | copy-start | bytes 786436

commit v5 on v4

--- a/solution.py
+++ b/solution.py
@@ -19,36 +19,35 @@
 
 
 def table_bases(total_lat, total_lon):
-    waves = np.arange(total_lon // 2)
-    cells = np.arange(total_lon)
-    lats = np.arange(total_lat)
-    group = np.arange(32)
+    cells = np.arange(total_lon // 2)
     fine = np.arange(16)
-    place, core = lats // 2, lats % 2
-    row_y, row_z, row_hi, row_lo = place // 32, place // 4 % 8, place // 2 % 2, place % 2
-    row = 16 * ((row_hi * 8 + row_y) * 2 + core) + 2 * row_z + row_lo
-    out = []
-    c, s = wave(16 * np.outer(group, cells), total_lon)
-    pc, ps = wave(np.outer(fine, cells), total_lon)
+    place, core = np.arange(total_lat // 2) // 2, np.arange(total_lat // 2) % 2
+    row = 16 * (place // 16 * 2 + core) + place % 16
+    lon_waves = np.arange(total_lon // 2).reshape(-1, 2).T.reshape(-1)
+    lat_waves = np.arange(total_lat).reshape(-1, 2).T.reshape(2, -1)
+    c, s = wave(np.outer(lon_waves[::16], cells), total_lon)
+    pc, ps = wave(2 * np.outer(fine, cells), total_lon)
     p = np.stack([pc, -ps], axis=1).reshape(32, -1)
     q = np.stack([-ps, -pc], axis=1).reshape(32, -1)
-    out.append((c, s, p, q))
-    c, s = wave(16 * np.outer(group, np.repeat(row, 2)), total_lat)
-    pc, ps = wave(np.outer(fine, row), total_lat)
+    narrow = [(c, s, p, q)]
+    c, s = wave(np.outer(lat_waves.reshape(-1)[::16], np.repeat(row, 2)), total_lat)
+    pc, ps = wave(2 * np.outer(fine, row), total_lat)
     p = np.stack([np.stack([pc, ps], 2), np.stack([-ps, pc], 2)]).reshape(32, -1)
     q = np.stack([np.stack([-ps, pc], 2), np.stack([-pc, -ps], 2)]).reshape(32, -1)
-    out.append((c, s, p, q))
-    c, s = wave(np.outer(row[::16], np.tile(lats, 2)), total_lat)
-    pc, ps = wave(np.outer(row[:16], lats), total_lat)
-    p = np.stack([np.stack([pc, -ps], 1), np.stack([ps, pc], 1)], 1).reshape(32, -1)
-    q = np.stack([np.stack([-ps, -pc], 1), np.stack([pc, -ps], 1)], 1).reshape(32, -1)
-    out.append((c, s, p, q))
-    c, s = wave(32 * np.outer(group, np.repeat(waves, 2)), total_lon)
-    pc, ps = wave(np.outer(group, waves), total_lon)
+    narrow.append((c, s, p, q))
+    columns = np.stack([lat_waves, lat_waves], axis=1).reshape(-1)
+    c, s = wave(np.outer(np.tile(row[::16], 2), columns), total_lat)
+    pc, ps = wave(np.outer(row[:16], lat_waves), total_lat)
+    pc, ps = pc.reshape(16, 2, -1), ps.reshape(16, 2, -1)
+    p = np.stack([np.stack([pc, -ps], 2), np.stack([ps, pc], 2)], 1).reshape(32, -1)
+    q = np.stack([np.stack([-ps, -pc], 2), np.stack([pc, -ps], 2)], 1).reshape(32, -1)
+    broad = [(c, s, p, q)]
+    c, s = wave(np.outer(np.tile(cells[::32], 2), np.repeat(lon_waves, 2)), total_lon)
+    pc, ps = wave(np.outer(np.arange(32), lon_waves), total_lon)
     p = np.stack([pc, -ps], axis=2).reshape(32, -1)
     q = np.stack([-ps, -pc], axis=2).reshape(32, -1)
-    out.append((c, s, p, q))
-    return np.stack([np.stack(kind) for kind in out]).astype(np.float32)
+    broad.append((c, s, p, q))
+    return [np.array(t).astype(np.float32) for t in (narrow, broad)]
 
 
 def wide_order():
@@ -70,13 +69,15 @@
 
 def mixer_kernel(
     x_ref,
-    bases_hbm,
+    narrow_hbm,
+    broad_hbm,
     w1_hbm,
     b1_hbm,
     w2_hbm,
     b2_hbm,
     landed,
-    bases,
+    narrow,
+    broad,
     w1_ref,
     b1_ref,
     w2_ref,
@@ -87,6 +88,8 @@
     t4,
     swap,
     swap_back,
+    mix1,
+    mix2,
     line,
     spec,
     pair,
@@ -107,10 +110,12 @@
     x_hi, y, core = lat // 16, lax.rem(lat // 2, 8), lax.rem(lat, 2)
     z, x_lo = lon // 2, lax.rem(lon, 2)
     z_hi = lon // 8
-    norm = 1.0 / math.sqrt(t2.shape[0] // 2 * t1.shape[1])
+    norm = 1.0 / math.sqrt(t2.shape[0] // 2 * t4.shape[1])
 
     fetches = [
-        pltpu.make_async_copy(bases_hbm.at[n], bases.at[n], table_sem.at[n]) for n in range(4)
+        pltpu.make_async_copy(hbm.at[n], vmem.at[n], table_sem.at[2 * m + n])
+        for m, (hbm, vmem) in enumerate(((narrow_hbm, narrow), (broad_hbm, broad)))
+        for n in range(2)
     ] + [
         pltpu.make_async_copy(hbm, vmem, table_sem.at[4 + n])
         for n, (hbm, vmem) in enumerate(
@@ -122,21 +127,28 @@
 
     def build(n, table):
         fetches[n].wait()
+        bases = (narrow if n < 2 else broad).at[n % 2]
 
         def group(g, _):
-            c = bases[n, 0, pl.ds(g, 1), :]
-            s = bases[n, 1, pl.ds(g, 1), :]
+            c = bases[0, pl.ds(g, 1), :]
+            s = bases[1, pl.ds(g, 1), :]
             if n == 1:
                 for part in range(2):
                     near = pl.ds(16 * part, 16)
-                    block = c * bases[n, 2, near, :] + s * bases[n, 3, near, :]
-                    start = pl.multiple_of(512 * part + 16 * g, 16)
-                    table[pl.ds(start, 16), :] = block.astype(table.dtype)
+                    block = c * bases[2, near, :] + s * bases[3, near, :]
+                    start = 512 * (g // 16) + 256 * part + 16 * lax.rem(g, 16)
+                    table[pl.ds(pl.multiple_of(start, 16), 16), :] = block.astype(table.dtype)
             else:
-                table[aligned(g, 32), :] = (c * bases[n, 2] + s * bases[n, 3]).astype(table.dtype)
+                table[aligned(g, 32), :] = (c * bases[2] + s * bases[3]).astype(table.dtype)
             return 0
 
-        lax.fori_loop(0, 32, group, 0)
+        lax.fori_loop(0, 32 if n < 2 else 16, group, 0)
+
+    def join(w_ref, mix):
+        mix[:128, :128] = w_ref[0, 0]
+        mix[:128, 128:] = w_ref[1, 0]
+        mix[128:, :128] = -w_ref[1, 0]
+        mix[128:, 128:] = w_ref[0, 0]
 
     barrier = pltpu.get_barrier_semaphore()
 
@@ -194,12 +206,12 @@
     zs = [lax.rem(z + step, 8) for step in range(8)]
     his = [x_hi, 1 - x_hi]
     los = [x_lo, 1 - x_lo]
-    place = ((y * 8 + z) * 2 + x_hi) * 2 + x_lo
+    place = ((x_hi * 8 + y) * 8 + z) * 2 + x_lo
 
     def to_chips(slot, source, landing):
         keep(slot, source.at[aligned(place, 4)], landing.at[aligned(place, 4)])
         for dy, dz, dh, dl in wide_order():
-            other = ((ys[dy] * 8 + zs[dz]) * 2 + his[dh]) * 2 + los[dl]
+            other = ((his[dh] * 8 + ys[dy]) * 8 + zs[dz]) * 2 + los[dl]
             pltpu.make_async_remote_copy(
                 src_ref=source.at[aligned(other, 4)],
                 dst_ref=landing.at[aligned(place, 4)],
@@ -223,9 +235,15 @@
     swap_back[...] = jnp.where(row == source, 1.0, 0.0).astype(swap.dtype)
     arrived(0, line)
 
-    def half_of(which):
-        rows = pl.ds(pl.multiple_of(512 * which, 512), 512)
-        return jnp.dot(t1[rows, :], line[...], preferred_element_type=jnp.float32).astype(spec.dtype)
+    def fold(block, sign):
+        return (block[:512].astype(jnp.float32) + sign * block[512:].astype(jnp.float32)).astype(
+            block.dtype
+        )
+
+    def half_of(parity):
+        rows = pl.ds(pl.multiple_of(512 * parity, 512), 512)
+        operand = fold(line[...], (1 - 2 * parity).astype(jnp.float32))
+        return jnp.dot(t1[rows, :], operand, preferred_element_type=jnp.float32).astype(spec.dtype)
 
     spec[...] = half_of(1 - core)
     to_sibling(1, spec, pair.at[core])
@@ -241,32 +259,34 @@
     build(2, t3)
     for copy in fetches[4:]:
         copy.wait()
+    join(w1_ref, mix1)
+    join(w2_ref, mix2)
+    bias1 = jnp.concatenate([b1_ref[0], b1_ref[1]], axis=1)
+    bias2 = jnp.concatenate([b2_ref[0], b2_ref[1]], axis=1)
+    weight = jnp.where(lat + lon == 0, 0.5, 1.0)
     arrived(2, column)
-    spectrum = jnp.dot(t2[...], column[...], preferred_element_type=jnp.float32)
-    spectrum = (spectrum * norm).astype(jnp.bfloat16)
-
-    def product(left_re, left_im, w_ref):
-        w_re, w_im = w_ref[0, 0], w_ref[1, 0]
-        re = jnp.dot(left_re, w_re, preferred_element_type=jnp.float32) - jnp.dot(
-            left_im, w_im, preferred_element_type=jnp.float32
-        )
-        im = jnp.dot(left_im, w_re, preferred_element_type=jnp.float32) + jnp.dot(
-            left_re, w_im, preferred_element_type=jnp.float32
-        )
-        return re, im
 
     def shrink(v):
         return jnp.maximum(v - shrink_level, 0.0) + jnp.minimum(v + shrink_level, 0.0)
 
-    hid_re, hid_im = product(spectrum[:512], spectrum[512:], w1_ref)
-    act_re = jnp.maximum(hid_re + b1_ref[0], 0.0).astype(jnp.bfloat16)
-    act_im = jnp.maximum(hid_im + b1_ref[1], 0.0).astype(jnp.bfloat16)
-    out_re, out_im = product(act_re, act_im, w2_ref)
-    weight = jnp.where(lat + lon == 0, 0.5, 1.0)
-    mixed[:512] = (shrink(out_re + b2_ref[0]) * weight).astype(jnp.bfloat16)
-    mixed[512:] = (shrink(out_im + b2_ref[1]) * weight).astype(jnp.bfloat16)
-
-    back[...] = jnp.dot(t3[...], mixed[...], preferred_element_type=jnp.float32).astype(back.dtype)
+    for parity in range(2):
+        rows = pl.ds(512 * parity, 512)
+        spectrum = jnp.dot(
+            t2[rows, :], fold(column[...], 1.0 - 2.0 * parity), preferred_element_type=jnp.float32
+        )
+        spectrum = (spectrum * norm).astype(jnp.bfloat16)
+        spectrum = jnp.concatenate([spectrum[:256], spectrum[256:]], axis=1)
+        hidden = jnp.dot(spectrum, mix1[...], preferred_element_type=jnp.float32)
+        hidden = jnp.maximum(hidden + bias1, 0.0).astype(jnp.bfloat16)
+        result = jnp.dot(hidden, mix2[...], preferred_element_type=jnp.float32)
+        result = (shrink(result + bias2) * weight).astype(jnp.bfloat16)
+        mixed[512 * parity : 512 * parity + 256] = result[:, :128]
+        mixed[512 * parity + 256 : 512 * parity + 512] = result[:, 128:]
+
+    even = jnp.dot(t3[:, :512], mixed[:512], preferred_element_type=jnp.float32)
+    odd = jnp.dot(t3[:, 512:], mixed[512:], preferred_element_type=jnp.float32)
+    back[:512] = (even + odd).astype(back.dtype)
+    back[512:] = (even - odd).astype(back.dtype)
     to_chips(3, back, wide)
     build(3, t4)
     arrived(3, wide)
@@ -278,17 +298,18 @@
         pair_back[:, 128 * block : 128 * block + 128, :] = both
     to_sibling(4, pair_back.at[1 - core], waves)
 
-    def part_of(half, which, operand):
-        rows = pl.ds(pl.multiple_of(512 * half, 512), 512)
-        columns = pl.ds(pl.multiple_of(512 * which, 512), 512)
-        return jnp.dot(t4[rows, columns], operand, preferred_element_type=jnp.float32)
-
-    far = 1 - z_hi
-    held = [part_of(half, core, pair_back[core]) for half in (far, z_hi)]
+    def part_of(parity, operand):
+        columns = pl.ds(pl.multiple_of(512 * parity, 512), 512)
+        return jnp.dot(t4[:, columns], operand, preferred_element_type=jnp.float32)
+
+    held = part_of(core, pair_back[core])
     arrived(4, waves)
-    for turn, half in enumerate((far, z_hi)):
-        filtered = held[turn] + part_of(half, 1 - core, waves[...])
-        field[512 * turn : 512 * turn + 512, :] = (filtered * (2.0 * norm)).astype(field.dtype)
+    fresh = part_of(1 - core, waves[...])
+    for turn, half in enumerate((1 - z_hi, z_hi)):
+        sign = (1 - 2 * half).astype(jnp.float32)
+        scale = (1 - 2 * half * core).astype(jnp.float32) * (2.0 * norm)
+        filtered = (held + sign * fresh) * scale
+        field[512 * turn : 512 * turn + 512, :] = filtered.astype(field.dtype)
 
         def block_of(peer, turn=turn):
             return field.at[pl.ds(pl.multiple_of(512 * turn + 64 * lax.rem(peer, 8), 64), 64)]
@@ -314,22 +335,24 @@
     lat_rows, lon_cells, channels = features.shape
     lat_count, lon_count = lax.axis_size("lat"), lax.axis_size("lon")
     total_lat, total_lon = lat_rows * lat_count, lon_cells * lon_count
-    bases = jnp.asarray(table_bases(total_lat, total_lon))
+    narrow, broad = (jnp.asarray(t) for t in table_bases(total_lat, total_lon))
     hbm = pl.BlockSpec(memory_space=pltpu.HBM)
     half = jnp.bfloat16
     flat = pltpu.VMEM((1024, channels), half)
-    table = pltpu.VMEM((1024, 1024), half)
+    tables = [pltpu.VMEM(shape, half) for shape in [(1024, 512)] * 2 + [(512, 1024)] * 2]
     filtered = pl.pallas_call(
         mixer_kernel,
         out_shape=jax.ShapeDtypeStruct((lat_rows, lon_cells, channels), half),
-        in_specs=[hbm] * 6,
+        in_specs=[hbm] * 7,
         out_specs=pl.BlockSpec(memory_space=pltpu.VMEM),
         scratch_shapes=[
             pltpu.VMEM(a.shape, a.dtype)
-            for a in (bases, w_first, bias_first, w_second, bias_second)
+            for a in (narrow, broad, w_first, bias_first, w_second, bias_second)
         ]
-        + [table] * 4
+        + tables
         + [
+            pltpu.VMEM((256, 256), half),
+            pltpu.VMEM((256, 256), half),
             pltpu.VMEM((256, 256), half),
             pltpu.VMEM((256, 256), half),
             flat,
@@ -353,7 +376,7 @@
     )(
         *(
             pltpu.with_memory_space_constraint(a, pltpu.HBM)
-            for a in (features, bases, w_first, bias_first, w_second, bias_second)
+            for a in (features, narrow, broad, w_first, bias_first, w_second, bias_second)
         )
     )
     return (features.astype(jnp.float32) + filtered.astype(jnp.float32)).astype(features.dtype)

time: 61.5 us -> 59.4 us (0.966)
  Pallas kernels: 60.6 us -> 58.5 us
    pallas_call x1, Pallas kernels: 60.6 us -> 58.5 us  [body(): pl.pallas_call(mixer_kernel, out_shape=jax.ShapeDtypeStruct((lat_rows, lo...]
where the time goes in v5:
time: 59.4 us; the launch traced here: 59.3 us
  Pallas kernels  58.5 us (98%)
  other arithmetic  0.78 us (1%)
    pallas_call x1, Pallas kernels, body(): pl.pallas_call(mixer_kernel, out_shape=jax.ShapeDtypeStruct((lat_rows, lo...  58.5 us

profile of v5, /device:TPU:1, one launch (start us, length us, event | category | flops | bytes accessed | tf_op | source)
XLA Modules:
  0.0 59.3 jit_solution(323411257577381395)
XLA Ops:
  0.0 0.0 copy-start
  0.0 58.5 %shard_map.73 = bf16[16,64,128]{2,1,0:T(8,128)(2,1)S(1)} custom-call(bf16[16,64,128]{2,1,0:T(8,128)(2,1)} %x_ref.1, f32[2,4,32,512]{3,2,1,0:T(8,128)} %constant.4.clone.narrow_hbm, f32[2,4,32,1024]{3,2,1,0:T(8,128)} %constant.5.clone.broad_hbm, bf16[2,1,128,128]{3,2,1,0:T(8,128)(2,1)} %w1_hbm.1, f32[2,1,128]{2,1,0:T(1,128)} %b1_hbm.1, ...), custom_call_target="tpu_custom_call" | custom-call | tf_op jit(solution)/shard_map/pallas_call | solution.py:343
  58.5 0.0 copy-done
  58.5 0.8 %add_convert_fusion = bf16[16,64,128]{2,1,0:T(8,128)(2,1)} fusion(bf16[16,64,128]{2,1,0:T(8,128)(2,1)S(1)} %shard_map.73, bf16[16,64,128]{2,1,0:T(8,128)(2,1)S(1)} %copy-done), kind=kLoop, calls=%fused_computation | loop fusion | flops 524288 | bytes 786432 | tf_op jit(solution)/shard_map/convert_element_type | solution.py:382
Async XLA Ops:
  0.0 58.5 %copy-start = (bf16[16,64,128]{2,1,0:T(8,128)(2,1)S(1)}, bf16[16,64,128]{2,1,0:T(8,128)(2,1)}, u32[]{:S(2)}) copy-start(bf16[16,64,128]{2,1,0:T(8,128)(2,1)} %x_ref.1) | copy-start | bytes 786436

commit v6 on v5

--- a/solution.py
+++ b/solution.py
@@ -112,19 +112,6 @@
     z_hi = lon // 8
     norm = 1.0 / math.sqrt(t2.shape[0] // 2 * t4.shape[1])
 
-    fetches = [
-        pltpu.make_async_copy(hbm.at[n], vmem.at[n], table_sem.at[2 * m + n])
-        for m, (hbm, vmem) in enumerate(((narrow_hbm, narrow), (broad_hbm, broad)))
-        for n in range(2)
-    ] + [
-        pltpu.make_async_copy(hbm, vmem, table_sem.at[4 + n])
-        for n, (hbm, vmem) in enumerate(
-            ((w1_hbm, w1_ref), (b1_hbm, b1_ref), (w2_hbm, w2_ref), (b2_hbm, b2_ref))
-        )
-    ]
-    for copy in fetches:
-        copy.start()
-
     def build(n, table):
         fetches[n].wait()
         bases = (narrow if n < 2 else broad).at[n % 2]
@@ -166,6 +153,19 @@
     lax.fori_loop(1, 16, greet_lon, 0)
     lax.fori_loop(1, 16, greet_lat, 0)
     pl.semaphore_signal(barrier, inc=1, device_id={"lat": sibling}, device_id_type=MESH)
+    fetches = [
+        pltpu.make_async_copy(hbm.at[n], vmem.at[n], table_sem.at[2 * m + n])
+        for m, (hbm, vmem) in enumerate(((narrow_hbm, narrow), (broad_hbm, broad)))
+        for n in range(2)
+    ] + [
+        pltpu.make_async_copy(hbm, vmem, table_sem.at[4 + n])
+        for n, (hbm, vmem) in enumerate(
+            ((w1_hbm, w1_ref), (b1_hbm, b1_ref), (w2_hbm, w2_ref), (b2_hbm, b2_ref))
+        )
+    ]
+    for copy in fetches:
+        copy.start()
+
     pl.semaphore_wait(barrier, 31)
 
     def lon_peer(step):
@@ -309,7 +309,9 @@
         sign = (1 - 2 * half).astype(jnp.float32)
         scale = (1 - 2 * half * core).astype(jnp.float32) * (2.0 * norm)
         filtered = (held + sign * fresh) * scale
-        field[512 * turn : 512 * turn + 512, :] = filtered.astype(field.dtype)
+        cells = pl.ds(pl.multiple_of(512 * half, 512), 512)
+        total = line[cells, :].astype(jnp.float32) + filtered.astype(field.dtype).astype(jnp.float32)
+        field[512 * turn : 512 * turn + 512, :] = total.astype(field.dtype)
 
         def block_of(peer, turn=turn):
             return field.at[pl.ds(pl.multiple_of(512 * turn + 64 * lax.rem(peer, 8), 64), 64)]
@@ -340,7 +342,7 @@
     half = jnp.bfloat16
     flat = pltpu.VMEM((1024, channels), half)
     tables = [pltpu.VMEM(shape, half) for shape in [(1024, 512)] * 2 + [(512, 1024)] * 2]
-    filtered = pl.pallas_call(
+    return pl.pallas_call(
         mixer_kernel,
         out_shape=jax.ShapeDtypeStruct((lat_rows, lon_cells, channels), half),
         in_specs=[hbm] * 7,
@@ -379,7 +381,6 @@
             for a in (features, narrow, broad, w_first, bias_first, w_second, bias_second)
         )
     )
-    return (features.astype(jnp.float32) + filtered.astype(jnp.float32)).astype(features.dtype)
 
 
 def solution(mesh):

time: 59.4 us -> 59 us (level)
  other arithmetic: 0.78 us -> 0 us
  local copies, waits for them, and re-layouts: 0.01 us -> 0.71 us
    convert_element_type x1 -> x0, other arithmetic: 0.78 us -> none  [body(): (features.astype(jnp.float32) + filtered.astype(jnp.float32)).astype(feat...]
    unnamed x2 -> x1, local copies, waits for them, and re-layouts: 0.01 us -> 0.71 us
where the time goes in v6:
time: 59 us; the launch traced here: 58.9 us
  Pallas kernels  58.2 us (99%)
  local copies, waits for them, and re-layouts  0.71 us (1%)
    pallas_call x1, Pallas kernels, body(): pl.pallas_call(mixer_kernel, out_shape=jax.ShapeDtypeStruct((lat_rows, lo...  58.2 us

profile of v6, /device:TPU:1, one launch (start us, length us, event | category | flops | bytes accessed | tf_op | source)
XLA Modules:
  0.0 58.9 jit_solution(3779713232730120314)
XLA Ops:
  0.0 58.2 %shard_map.73 = bf16[16,64,128]{2,1,0:T(8,128)(2,1)S(1)} custom-call(bf16[16,64,128]{2,1,0:T(8,128)(2,1)} %x_ref.1, f32[2,4,32,512]{3,2,1,0:T(8,128)} %constant.4.clone.narrow_hbm, f32[2,4,32,1024]{3,2,1,0:T(8,128)} %constant.5.clone.broad_hbm, bf16[2,1,128,128]{3,2,1,0:T(8,128)(2,1)} %w1_hbm.1, f32[2,1,128]{2,1,0:T(1,128)} %b1_hbm.1, ...), custom_call_target="tpu_custom_call" | custom-call | tf_op jit(solution)/shard_map/pallas_call | solution.py:345
  58.2 0.7 %copy.9 = bf16[16,64,128]{2,1,0:T(8,128)(2,1)} copy(bf16[16,64,128]{2,1,0:T(8,128)(2,1)S(1)} %shard_map.73) | data formatting | bytes 524288

commit v7 on v6

--- a/solution.py
+++ b/solution.py
@@ -153,19 +153,6 @@
     lax.fori_loop(1, 16, greet_lon, 0)
     lax.fori_loop(1, 16, greet_lat, 0)
     pl.semaphore_signal(barrier, inc=1, device_id={"lat": sibling}, device_id_type=MESH)
-    fetches = [
-        pltpu.make_async_copy(hbm.at[n], vmem.at[n], table_sem.at[2 * m + n])
-        for m, (hbm, vmem) in enumerate(((narrow_hbm, narrow), (broad_hbm, broad)))
-        for n in range(2)
-    ] + [
-        pltpu.make_async_copy(hbm, vmem, table_sem.at[4 + n])
-        for n, (hbm, vmem) in enumerate(
-            ((w1_hbm, w1_ref), (b1_hbm, b1_ref), (w2_hbm, w2_ref), (b2_hbm, b2_ref))
-        )
-    ]
-    for copy in fetches:
-        copy.start()
-
     pl.semaphore_wait(barrier, 31)
 
     def lon_peer(step):
@@ -226,6 +213,19 @@
 
     keep(0, x_ref.at[lon], line.at[aligned(lon, 64)])
     push(0, "lon", (0, 15), lon_peer, lambda p: x_ref.at[p], line.at[aligned(lon, 64)])
+    fetches = [
+        pltpu.make_async_copy(hbm.at[n], vmem.at[n], table_sem.at[2 * m + n])
+        for m, (hbm, vmem) in enumerate(((narrow_hbm, narrow), (broad_hbm, broad)))
+        for n in range(2)
+    ] + [
+        pltpu.make_async_copy(hbm, vmem, table_sem.at[4 + n])
+        for n, (hbm, vmem) in enumerate(
+            ((w1_hbm, w1_ref), (b1_hbm, b1_ref), (w2_hbm, w2_ref), (b2_hbm, b2_ref))
+        )
+    ]
+    for copy in fetches:
+        copy.start()
+
     build(0, t1)
     row = lax.broadcasted_iota(jnp.int32, swap.shape, 0)
     col = lax.broadcasted_iota(jnp.int32, swap.shape, 1)

time: 59 us -> 59 us (level)
  no operation moved by 1% of the time
where the time goes in v7:
time: 59 us; the launch traced here: 58.9 us
  Pallas kernels  58.2 us (99%)
  local copies, waits for them, and re-layouts  0.71 us (1%)
    pallas_call x1, Pallas kernels, body(): pl.pallas_call(mixer_kernel, out_shape=jax.ShapeDtypeStruct((lat_rows, lo...  58.2 us

profile of v7, /device:TPU:1, one launch (start us, length us, event | category | flops | bytes accessed | tf_op | source)
XLA Modules:
  0.0 58.9 jit_solution(3566071181612848983)
XLA Ops:
  0.0 58.2 %shard_map.73 = bf16[16,64,128]{2,1,0:T(8,128)(2,1)S(1)} custom-call(bf16[16,64,128]{2,1,0:T(8,128)(2,1)} %x_ref.1, f32[2,4,32,512]{3,2,1,0:T(8,128)} %constant.4.clone.narrow_hbm, f32[2,4,32,1024]{3,2,1,0:T(8,128)} %constant.5.clone.broad_hbm, bf16[2,1,128,128]{3,2,1,0:T(8,128)(2,1)} %w1_hbm.1, f32[2,1,128]{2,1,0:T(1,128)} %b1_hbm.1, ...), custom_call_target="tpu_custom_call" | custom-call | tf_op jit(solution)/shard_map/pallas_call | solution.py:345
  58.2 0.7 %copy.9 = bf16[16,64,128]{2,1,0:T(8,128)(2,1)} copy(bf16[16,64,128]{2,1,0:T(8,128)(2,1)S(1)} %shard_map.73) | data formatting | bytes 524288
